TPU v7x, 32 devices: a whole 2x2x4 slice. The times are simulated.
32 devices in a mesh: line: 2 (over y), bin: 16 (over z, x, core).
Axes of the slice: x: 2, y: 2, z: 4, core: 2. Of those that a mesh axis runs over, the one named last changes fastest.
Arguments:
- predicted: bfloat16 [4096, 2048], P(('line', 'bin')), parts along dimension 0, may hold values from -1200 to 1200
- observed: float32 [4096, 2048], P(('line', 'bin')), parts along dimension 0, may hold values from -1200 to 1200
- data_weight: float32 [4096, 2048], P(('line', 'bin')), parts along dimension 0, may hold values from 0.5 to 2
- bin_ids: int32 [4096], P(('line', 'bin')), parts along dimension 0, may hold values from 0 to 31, as said below
- offset_slots: int32 [4096], P(('line', 'bin')), parts along dimension 0, may hold values from 0 to 63, as said below
- conv_in: bfloat16 [3, 3, 48], replicated, may hold values from -2 to 2
- conv_mid: bfloat16 [3, 3, 48, 48], replicated, may hold values from -0.3125 to 0.3125
- conv_out: bfloat16 [3, 3, 48], replicated, may hold values from -0.3125 to 0.3125
Outputs:
- residual_traces: bfloat16 [4096, 2048], P(('line', 'bin')), parts along dimension 0
There are 2 independent parts, one for each index of `line`. A program takes and returns all parts, laid end to end along the dimension named above; an argument that names none is the same for every part. Nothing has to cross between parts.
Inputs may be any that keep to these rules, and one draw needn't show every extreme that they name: `bin_ids`: bin b belongs to index b // 2 of bin. The traces of one device go at most 16 to one owner and at most 8 to one bin, both reached in every draw. Taken by owner index minus the sender's index, modulo the devices of bin, every device sends the same counts. Every owner receives exactly 128 traces, 64 in each of its bins. `offset_slots`: no two traces have the same bin and slot.
All inputs are finite; a program needn't handle non-finite values.
Results may differ from a plain program's by a relative error of at most 0.0065.
Values may be sent and summed in bfloat16 or wider, within the bound.
A program may use at most 256 MiB of HBM per device.

v0:
```python
import jax
import jax.numpy as jnp
from jax import lax
from jax.sharding import PartitionSpec as P

OFFS = 64


rim_width = 6
window_span = 512
kept_span = 500


def shifted(values, along_offset, along_time):
    last = values.ndim - 1
    span_x = values.shape[-2]
    span_t = values.shape[-1]
    pad_x = abs(along_offset)
    pad_t = abs(along_time)
    widths = [(0, 0)] * (values.ndim - 2) + [(pad_x, pad_x), (pad_t, pad_t)]
    padded = jnp.pad(values, widths)
    padded = lax.slice_in_dim(
        padded, pad_x + along_offset, pad_x + along_offset + span_x, axis=last - 1
    )
    return lax.slice_in_dim(padded, pad_t + along_time, pad_t + along_time + span_t, axis=last)


def filter_panels(panels, conv_in, conv_mid, conv_out):
    bin_count, offsets, samples = panels.shape
    blocks = -(-samples // kept_span)
    extent = blocks * kept_span
    padded = jnp.pad(panels, ((0, 0), (0, 0), (rim_width, extent - samples + rim_width)))
    channels = conv_in.shape[-1]

    def one_block(block, result):
        start = block * kept_span
        window = lax.dynamic_slice_in_dim(padded, start, window_span, 2)
        times = start - rim_width + jnp.arange(window_span, dtype=jnp.int32)
        inside = (times >= 0) & (times < samples)
        values = window.astype(jnp.float32)
        first_sum = jnp.zeros((channels,) + values.shape, jnp.float32)
        for row_tap in range(3):
            for time_tap in range(3):
                weights = conv_in[row_tap, time_tap].astype(jnp.float32)
                first_sum = (
                    first_sum
                    + weights[:, None, None, None]
                    * shifted(values, row_tap - 1, time_tap - 1)[None]
                )
        first_hidden = jnp.where(inside, jax.nn.silu(first_sum), 0.0).astype(jnp.bfloat16)
        second_sum = jnp.zeros((channels,) + values.shape, jnp.float32)
        for row_tap in range(3):
            for time_tap in range(3):
                second_sum = second_sum + jnp.einsum(
                    "io,inxt->onxt",
                    conv_mid[row_tap, time_tap],
                    shifted(first_hidden, 2 * (row_tap - 1), 4 * (time_tap - 1)),
                    preferred_element_type=jnp.float32,
                )
        second_hidden = jnp.where(
            inside, first_hidden.astype(jnp.float32) + jax.nn.silu(second_sum), 0.0
        ).astype(jnp.bfloat16)
        third_sum = jnp.zeros(values.shape, jnp.float32)
        for row_tap in range(3):
            for time_tap in range(3):
                third_sum = third_sum + jnp.einsum(
                    "i,inxt->nxt",
                    conv_out[row_tap, time_tap],
                    shifted(second_hidden, row_tap - 1, time_tap - 1),
                    preferred_element_type=jnp.float32,
                )
        output = (values + third_sum).astype(jnp.bfloat16)
        piece = output[:, :, rim_width : rim_width + kept_span]
        return lax.dynamic_update_slice_in_dim(result, piece, start, 2)

    result = jnp.zeros((bin_count, offsets, extent), jnp.bfloat16)
    result = lax.fori_loop(0, blocks, one_block, result)
    return result[:, :, :samples]


def local(predicted, observed, data_weight, bin_ids, offset_slots, conv_in, conv_mid, conv_out):
    tr_dev, samples = predicted.shape
    owners = lax.axis_size("bin")
    bin_dev = tr_dev // OFFS
    capacity = max(bin_dev, 2 * tr_dev // owners)
    owner_dev = bin_ids // bin_dev
    local_bin = bin_ids % bin_dev
    row_index = jnp.arange(tr_dev, dtype=jnp.int32)
    earlier = row_index[None, :] < row_index[:, None]
    same_owner = owner_dev[:, None] == owner_dev[None, :]
    position = jnp.sum((same_owner & earlier).astype(jnp.int32), axis=1)
    send_slot = owner_dev * capacity + position
    panel_cell = local_bin * OFFS + offset_slots
    outgoing = (
        jnp.zeros((owners * capacity, samples), jnp.bfloat16)
        .at[send_slot]
        .set(predicted)
        .reshape(owners, capacity, samples)
    )
    outgoing_cells = (
        jnp.full((owners * capacity,), -1, jnp.int32)
        .at[send_slot]
        .set(panel_cell)
        .reshape(owners, capacity)
    )
    arrived, arrived_cells = (
        lax.all_to_all(outgoing, "bin", split_axis=0, concat_axis=0, tiled=True),
        lax.all_to_all(outgoing_cells, "bin", split_axis=0, concat_axis=0, tiled=True),
    )
    flat_cells = arrived_cells.reshape(-1)
    filled = flat_cells >= 0
    target = jnp.where(filled, flat_cells, bin_dev * OFFS)
    panels = (
        jnp.zeros((bin_dev * OFFS, samples), jnp.bfloat16)
        .at[target]
        .set(arrived.reshape(-1, samples), mode="drop")
        .reshape(bin_dev, OFFS, samples)
    )
    filtered = filter_panels(panels, conv_in, conv_mid, conv_out).reshape(bin_dev * OFFS, samples)
    answer = jnp.where(
        filled[:, None], filtered[jnp.where(filled, flat_cells, 0)], jnp.zeros((), jnp.bfloat16)
    ).reshape(owners, capacity, samples)
    returned = lax.all_to_all(answer, "bin", split_axis=0, concat_axis=0, tiled=True)
    own_rows = returned.reshape(-1, samples)[send_slot]
    misfit = data_weight * (own_rows.astype(jnp.float32) - observed)
    misfit_total = lax.psum(jnp.sum(misfit * misfit), "bin")
    mean_square = misfit_total / (tr_dev * owners * samples)
    return (misfit * lax.rsqrt(mean_square + 1e-05)).astype(jnp.bfloat16)


def solution(mesh):
    in_specs = (
        P(("line", "bin"), None),
        P(("line", "bin"), None),
        P(("line", "bin"), None),
        P(("line", "bin")),
        P(("line", "bin")),
        P(),
        P(),
        P(),
    )
    out_specs = P(("line", "bin"), None)
    return jax.shard_map(local, mesh=mesh, in_specs=in_specs, out_specs=out_specs, check_vma=False)
```

profile of v0, /device:TPU:0, one launch (start us, length us, event | category | flops | bytes accessed | tf_op | source)
XLA Modules:
  0.0 748.5 jit_solution(1214765087645335547)
XLA Ops:
  2.6 7.4 all-to-all-start
  23.4 19.4 %all-to-all-done.1 = bf16[16,16,2048]{2,1,0:T(8,128)(2,1)S(1)} async-done(((bf16[16,16,2048]{2,1,0:T(8,128)(2,1)}), bf16[16,16,2048]{2,1,0:T(8,128)(2,1)S(1)}, u32[]{:S(2)}, u32[]{:S(2)}) %all-to-all-start.1) | async-done | bytes 1048608 | tf_op jit(solution)/shard_map/all_to_all | solution.py:107
  47.0 626.1 %while.15 = (s32[]{:T(128)}, bf16[2,64,2500]{2,1,0:T(8,128)(2,1)}, bf16[2,64,2512]{2,1,0:T(8,128)(2,1)}, bf16[3,3,48]{2,1,0:T(4,128)(2,1)}, bf16[3,3,48,48]{2,3,...) while((s32[]{:T(128)}, bf16[2,64,2500]{2,1,0:T(8,128)(2,1)}, ...), condition=%wide.region_5.6_spmd, body=%wide.region_4.5_spmd.sunk | while | flops 3042436608 | bytes 363944288 | solution.py:77
  73.0 10.1 %select_convert_fusion.5 = bf16[48,2,64,512]{3,0,2,1:T(8,128)(2,1)S(1)} fusion(f32[2,64,512]{2,1,0:T(8,128)S(1)} %get-tuple-element.287, f32[48]{0:T(128)S(1)} %get-tuple-element.288, f32[2,64,512]{2,1,0:T(8,128)S(1)} %get-tuple-element.289, f32[48]{0:T(128)S(1)} %get-tuple-element.290, f32[2,64,512]{2,1,0:T(8,128)S(1)} %get-tuple-element.291, ...), kind=kLoop, calls=%fused_computation.12.clone.3 | loop fusion | flops 72351744 | bytes 8652992 | tf_op jit(solution)/shard_map/while/body/eval_jaxpr/convert_element_type | solution.py:50
  83.1 5.6 fusion.167
  88.7 5.6 fusion.166
  110.8 5.6 fusion.162
  122.0 5.6 fusion.160
  127.6 39.4 %fusion.168 = bf16[48,2,64,512]{3,0,2,1:T(8,128)(2,1)} fusion(f32[2,64,512,48]{2,3,1,0:T(8,128)} %fusion.160, f32[2,64,512,48]{2,3,1,0:T(8,128)} %fusion.161, f32[2,64,512,48]{2,3,1,0:T(8,128)} %fusion.162, f32[2,64,512,48]{2,3,1,0:T(8,128)} %fusion.163, f32[2,64,512,48]{2,3,1,0:T(8,128)} %fusion.164, f32[2,64,512,48]{2,3,1,0:T(8,128)} %fusion.165, ...), kind=kOutput, calls=%fused_computation.13.clone.1 | convolution fusion | flops 497025024 | bytes 111695872 | tf_op jit(solution)/shard_map/while/body/eval_jaxpr/io,inxt->onxt/dot_general | solution.py:54
  193.1 10.1 %select_convert_fusion.5 = bf16[48,2,64,512]{3,0,2,1:T(8,128)(2,1)S(1)} fusion(f32[2,64,512]{2,1,0:T(8,128)S(1)} %get-tuple-element.287, f32[48]{0:T(128)S(1)} %get-tuple-element.288, f32[2,64,512]{2,1,0:T(8,128)S(1)} %get-tuple-element.289, f32[48]{0:T(128)S(1)} %get-tuple-element.290, f32[2,64,512]{2,1,0:T(8,128)S(1)} %get-tuple-element.291, ...), kind=kLoop, calls=%fused_computation.12.clone.3 | loop fusion | flops 72351744 | bytes 8652992 | tf_op jit(solution)/shard_map/while/body/eval_jaxpr/convert_element_type | solution.py:50
  203.2 5.6 fusion.167
  230.9 5.6 fusion.162
  242.1 5.6 fusion.160
  247.7 39.4 %fusion.168 = bf16[48,2,64,512]{3,0,2,1:T(8,128)(2,1)} fusion(f32[2,64,512,48]{2,3,1,0:T(8,128)} %fusion.160, f32[2,64,512,48]{2,3,1,0:T(8,128)} %fusion.161, f32[2,64,512,48]{2,3,1,0:T(8,128)} %fusion.162, f32[2,64,512,48]{2,3,1,0:T(8,128)} %fusion.163, f32[2,64,512,48]{2,3,1,0:T(8,128)} %fusion.164, f32[2,64,512,48]{2,3,1,0:T(8,128)} %fusion.165, ...), kind=kOutput, calls=%fused_computation.13.clone.1 | convolution fusion | flops 497025024 | bytes 111695872 | tf_op jit(solution)/shard_map/while/body/eval_jaxpr/io,inxt->onxt/dot_general | solution.py:54
  313.7 10.1 %select_convert_fusion.5 = bf16[48,2,64,512]{3,0,2,1:T(8,128)(2,1)S(1)} fusion(f32[2,64,512]{2,1,0:T(8,128)S(1)} %get-tuple-element.287, f32[48]{0:T(128)S(1)} %get-tuple-element.288, f32[2,64,512]{2,1,0:T(8,128)S(1)} %get-tuple-element.289, f32[48]{0:T(128)S(1)} %get-tuple-element.290, f32[2,64,512]{2,1,0:T(8,128)S(1)} %get-tuple-element.291, ...), kind=kLoop, calls=%fused_computation.12.clone.3 | loop fusion | flops 72351744 | bytes 8652992 | tf_op jit(solution)/shard_map/while/body/eval_jaxpr/convert_element_type | solution.py:50
  323.8 5.6 fusion.167
  351.5 5.6 fusion.162
  362.7 5.6 fusion.160
  368.3 39.4 %fusion.168 = bf16[48,2,64,512]{3,0,2,1:T(8,128)(2,1)} fusion(f32[2,64,512,48]{2,3,1,0:T(8,128)} %fusion.160, f32[2,64,512,48]{2,3,1,0:T(8,128)} %fusion.161, f32[2,64,512,48]{2,3,1,0:T(8,128)} %fusion.162, f32[2,64,512,48]{2,3,1,0:T(8,128)} %fusion.163, f32[2,64,512,48]{2,3,1,0:T(8,128)} %fusion.164, f32[2,64,512,48]{2,3,1,0:T(8,128)} %fusion.165, ...), kind=kOutput, calls=%fused_computation.13.clone.1 | convolution fusion | flops 497025024 | bytes 111695872 | tf_op jit(solution)/shard_map/while/body/eval_jaxpr/io,inxt->onxt/dot_general | solution.py:54
  434.3 10.1 %select_convert_fusion.5 = bf16[48,2,64,512]{3,0,2,1:T(8,128)(2,1)S(1)} fusion(f32[2,64,512]{2,1,0:T(8,128)S(1)} %get-tuple-element.287, f32[48]{0:T(128)S(1)} %get-tuple-element.288, f32[2,64,512]{2,1,0:T(8,128)S(1)} %get-tuple-element.289, f32[48]{0:T(128)S(1)} %get-tuple-element.290, f32[2,64,512]{2,1,0:T(8,128)S(1)} %get-tuple-element.291, ...), kind=kLoop, calls=%fused_computation.12.clone.3 | loop fusion | flops 72351744 | bytes 8652992 | tf_op jit(solution)/shard_map/while/body/eval_jaxpr/convert_element_type | solution.py:50
  444.4 5.6 fusion.167
  472.1 5.6 fusion.162
  483.3 5.6 fusion.160
  488.9 39.4 %fusion.168 = bf16[48,2,64,512]{3,0,2,1:T(8,128)(2,1)} fusion(f32[2,64,512,48]{2,3,1,0:T(8,128)} %fusion.160, f32[2,64,512,48]{2,3,1,0:T(8,128)} %fusion.161, f32[2,64,512,48]{2,3,1,0:T(8,128)} %fusion.162, f32[2,64,512,48]{2,3,1,0:T(8,128)} %fusion.163, f32[2,64,512,48]{2,3,1,0:T(8,128)} %fusion.164, f32[2,64,512,48]{2,3,1,0:T(8,128)} %fusion.165, ...), kind=kOutput, calls=%fused_computation.13.clone.1 | convolution fusion | flops 497025024 | bytes 111695872 | tf_op jit(solution)/shard_map/while/body/eval_jaxpr/io,inxt->onxt/dot_general | solution.py:54
  554.9 10.1 %select_convert_fusion.5 = bf16[48,2,64,512]{3,0,2,1:T(8,128)(2,1)S(1)} fusion(f32[2,64,512]{2,1,0:T(8,128)S(1)} %get-tuple-element.287, f32[48]{0:T(128)S(1)} %get-tuple-element.288, f32[2,64,512]{2,1,0:T(8,128)S(1)} %get-tuple-element.289, f32[48]{0:T(128)S(1)} %get-tuple-element.290, f32[2,64,512]{2,1,0:T(8,128)S(1)} %get-tuple-element.291, ...), kind=kLoop, calls=%fused_computation.12.clone.3 | loop fusion | flops 72351744 | bytes 8652992 | tf_op jit(solution)/shard_map/while/body/eval_jaxpr/convert_element_type | solution.py:50
  565.0 5.6 fusion.167
  592.7 5.6 fusion.162
  603.9 5.6 fusion.160
  609.5 39.4 %fusion.168 = bf16[48,2,64,512]{3,0,2,1:T(8,128)(2,1)} fusion(f32[2,64,512,48]{2,3,1,0:T(8,128)} %fusion.160, f32[2,64,512,48]{2,3,1,0:T(8,128)} %fusion.161, f32[2,64,512,48]{2,3,1,0:T(8,128)} %fusion.162, f32[2,64,512,48]{2,3,1,0:T(8,128)} %fusion.163, f32[2,64,512,48]{2,3,1,0:T(8,128)} %fusion.164, f32[2,64,512,48]{2,3,1,0:T(8,128)} %fusion.165, ...), kind=kOutput, calls=%fused_computation.13.clone.1 | convolution fusion | flops 497025024 | bytes 111695872 | tf_op jit(solution)/shard_map/while/body/eval_jaxpr/io,inxt->onxt/dot_general | solution.py:54
  676.9 6.8 all-to-all-start.2
  683.7 22.9 %all-to-all-done.2 = bf16[16,16,2048]{2,1,0:T(8,128)(2,1)S(1)} async-done(((bf16[16,16,2048]{2,1,0:T(8,128)(2,1)}), bf16[16,16,2048]{2,1,0:T(8,128)(2,1)S(1)}, u32[]{:S(2)}, u32[]{:S(2)}) %all-to-all-start.2) | async-done | bytes 1048608 | tf_op jit(solution)/shard_map/all_to_all | solution.py:123
  709.7 35.5 %psum.7 = f32[]{:T(128)} all-reduce(f32[]{:T(128)} %multiply_reduce_fusion), channel_id=1, replica_groups=mesh['line'=2,'bin'=16] {'bin'}, use_global_device_ids=true, to_apply=%region_7.8 | all-reduce | flops 1 | bytes 8 | tf_op jit(solution)/shard_map/psum | solution.py:126
  (167 shorter events, 293.9 us)
Async XLA Ops:
  0.9 20.1 %copy-start.4 = (s32[128]{0:T(128)}, s32[128]{0:T(128)S(1)}, u32[]{:S(2)}) copy-start(s32[128]{0:T(128)S(1)} %compare_select_fusion.4) | copy-start | bytes 1540
  2.6 13.7 %all-to-all-start = ((s32[16,1,16]{2,1,0:T(1,128)}), s32[16,1,16]{2,1,0:T(1,128)S(1)}, u32[]{:S(2)}, u32[]{:S(2)}) async-start(s32[16,1,16]{2,1,0:T(1,128)} %all_to_all.12), calls=%async_computation | async-start | bytes 16384 | tf_op jit(solution)/shard_map/all_to_all | solution.py:108
  16.3 26.6 %all-to-all-start.1 = ((bf16[16,16,2048]{2,1,0:T(8,128)(2,1)}), bf16[16,16,2048]{2,1,0:T(8,128)(2,1)S(1)}, u32[]{:S(2)}, u32[]{:S(2)}) async-start(bf16[16,16,2048]{2,1,0:T(8,128)(2,1)} %bitcast.76), calls=%async_computation.1 | async-start | bytes 2097152 | tf_op jit(solution)/shard_map/all_to_all | solution.py:107
  47.0 628.8 %copy-start.3 = (pred[16,16]{1,0:T(8,128)(4,1)S(1)}, pred[16,16]{1,0:T(8,128)(4,1)}, u32[]{:S(2)}) copy-start(pred[16,16]{1,0:T(8,128)(4,1)} %compare_bitcast_fusion) | copy-start | bytes 772
  127.6 39.5 %copy-start.2 = (bf16[3,3,48]{2,1,0:T(4,128)(2,1)S(1)}, bf16[3,3,48]{2,1,0:T(4,128)(2,1)}, u32[]{:S(2)}) copy-start(bf16[3,3,48]{2,1,0:T(4,128)(2,1)} %get-tuple-element.337) | copy-start | bytes 2596 | tf_op jit(solution)/shard_map/while
  167.0 8.8 %copy-start = (bf16[48,2,64,512]{3,0,2,1:T(8,128)(2,1)S(1)}, bf16[48,2,64,512]{3,0,2,1:T(8,128)(2,1)}, u32[]{:S(2)}) copy-start(bf16[48,2,64,512]{3,0,2,1:T(8,128)(2,1)} %fusion.168) | copy-start | bytes 18874372 | tf_op jit(solution)/shard_map/while
  247.7 39.5 %copy-start.2 = (bf16[3,3,48]{2,1,0:T(4,128)(2,1)S(1)}, bf16[3,3,48]{2,1,0:T(4,128)(2,1)}, u32[]{:S(2)}) copy-start(bf16[3,3,48]{2,1,0:T(4,128)(2,1)} %get-tuple-element.337) | copy-start | bytes 2596 | tf_op jit(solution)/shard_map/while
  287.2 8.8 %copy-start = (bf16[48,2,64,512]{3,0,2,1:T(8,128)(2,1)S(1)}, bf16[48,2,64,512]{3,0,2,1:T(8,128)(2,1)}, u32[]{:S(2)}) copy-start(bf16[48,2,64,512]{3,0,2,1:T(8,128)(2,1)} %fusion.168) | copy-start | bytes 18874372 | tf_op jit(solution)/shard_map/while
  368.3 39.5 %copy-start.2 = (bf16[3,3,48]{2,1,0:T(4,128)(2,1)S(1)}, bf16[3,3,48]{2,1,0:T(4,128)(2,1)}, u32[]{:S(2)}) copy-start(bf16[3,3,48]{2,1,0:T(4,128)(2,1)} %get-tuple-element.337) | copy-start | bytes 2596 | tf_op jit(solution)/shard_map/while
  407.8 8.8 %copy-start = (bf16[48,2,64,512]{3,0,2,1:T(8,128)(2,1)S(1)}, bf16[48,2,64,512]{3,0,2,1:T(8,128)(2,1)}, u32[]{:S(2)}) copy-start(bf16[48,2,64,512]{3,0,2,1:T(8,128)(2,1)} %fusion.168) | copy-start | bytes 18874372 | tf_op jit(solution)/shard_map/while
  488.9 39.5 %copy-start.2 = (bf16[3,3,48]{2,1,0:T(4,128)(2,1)S(1)}, bf16[3,3,48]{2,1,0:T(4,128)(2,1)}, u32[]{:S(2)}) copy-start(bf16[3,3,48]{2,1,0:T(4,128)(2,1)} %get-tuple-element.337) | copy-start | bytes 2596 | tf_op jit(solution)/shard_map/while
  528.4 8.8 %copy-start = (bf16[48,2,64,512]{3,0,2,1:T(8,128)(2,1)S(1)}, bf16[48,2,64,512]{3,0,2,1:T(8,128)(2,1)}, u32[]{:S(2)}) copy-start(bf16[48,2,64,512]{3,0,2,1:T(8,128)(2,1)} %fusion.168) | copy-start | bytes 18874372 | tf_op jit(solution)/shard_map/while
  609.5 39.4 %copy-start.2 = (bf16[3,3,48]{2,1,0:T(4,128)(2,1)S(1)}, bf16[3,3,48]{2,1,0:T(4,128)(2,1)}, u32[]{:S(2)}) copy-start(bf16[3,3,48]{2,1,0:T(4,128)(2,1)} %get-tuple-element.337) | copy-start | bytes 2596 | tf_op jit(solution)/shard_map/while
  649.0 8.8 %copy-start = (bf16[48,2,64,512]{3,0,2,1:T(8,128)(2,1)S(1)}, bf16[48,2,64,512]{3,0,2,1:T(8,128)(2,1)}, u32[]{:S(2)}) copy-start(bf16[48,2,64,512]{3,0,2,1:T(8,128)(2,1)} %fusion.168) | copy-start | bytes 18874372 | tf_op jit(solution)/shard_map/while
  673.1 10.6 %copy-start.5 = (s32[128]{0:T(128)S(1)}, s32[128]{0:T(128)}, u32[]{:S(2)}) copy-start(s32[128]{0:T(128)} %copy-done.4) | copy-start | bytes 1540
  673.1 34.5 %copy-start.1 = (f32[128,2048]{1,0:T(8,128)S(1)}, f32[128,2048]{1,0:T(8,128)}, u32[]{:S(2)}) copy-start(f32[128,2048]{1,0:T(8,128)} %param.12) | copy-start | bytes 3145732
  676.9 29.8 %all-to-all-start.2 = ((bf16[16,16,2048]{2,1,0:T(8,128)(2,1)}), bf16[16,16,2048]{2,1,0:T(8,128)(2,1)S(1)}, u32[]{:S(2)}, u32[]{:S(2)}) async-start(bf16[16,16,2048]{2,1,0:T(8,128)(2,1)} %broadcast_select_fusion), calls=%async_computation.2 | async-start | bytes 2097152 | tf_op jit(solution)/shard_map/all_to_all | solution.py:123
where the time goes:
time: 753 us; the launch traced here: 748 us
  matrix products  526 us (70%)
  other arithmetic  71 us (9%)
  waiting for transfers between devices  45.7 us (6%)
  blocking collectives  35.5 us (5%)
  local copies, waits for them, and re-layouts  27.4 us (4%)
  loops' own time  24 us (3%)
  starting transfers between devices  17.8 us (2%)
    dot_general x45, matrix products, one_block(): jnp.einsum('io,inxt->onxt', conv_mid[row_tap, time_tap], shifted(first_hi...  420 us
    dot_general x45, matrix products, one_block(): jnp.einsum('i,inxt->nxt', conv_out[row_tap, time_tap], shifted(second_hid...  106 us
    convert_element_type x5, other arithmetic, one_block(): jnp.where(inside, jax.nn.silu(first_sum), 0.0).astype(jnp.bfloat16)  50.5 us
    psum x1, blocking collectives, local(): misfit_total = lax.psum(jnp.sum(misfit * misfit), 'bin')  35.5 us
    another operation x1, loops' own time, filter_panels(): result = lax.fori_loop(0, blocks, one_block, result)  24 us
    all_to_all x1, waiting for transfers between devices, local(): lax.all_to_all(answer, 'bin', split_axis=0, concat_axis=0, tiled=True)  22.9 us
    all_to_all x1, waiting for transfers between devices, local(): lax.all_to_all(outgoing, 'bin', split_axis=0, concat_axis=0, tiled=True)  19.4 us
  transfers between devices with their start and end apart: 3, of which 3 were waited for; matrix products, arithmetic and copies ran while one was open for 1% of the time, Pallas kernels for 0%

commit v1 on v0

v1 whole, which is shorter than its diff:
```python
import jax
import jax.numpy as jnp
from jax import lax
from jax.experimental import pallas as pl
from jax.experimental.pallas import tpu as pltpu
from jax.sharding import PartitionSpec as P

OFFS = 64
CHAN = 48
SEGS = 8
HALF = (OFFS // 2) * CHAN
WIDE = HALF + 256
TILE = 256


def kernel_body(
    span, chunk_a, chunk_b, p3_ref, w_in_ref, w_mid_ref, w_out_ref, out_ref, h1_ref, z_ref
):
    blk = 2 * SEGS
    n_first = (span + 10) * blk
    n_second = (span + 2) * blk
    tiles = HALF // TILE
    zero_cols = jnp.zeros((n_first, 128), jnp.bfloat16)
    for parity in range(2):
        h1_ref[:, pl.ds(parity * WIDE, 128)] = zero_cols
        h1_ref[:, pl.ds(parity * WIDE + 128 + HALF, 128)] = zero_cols

    @pl.loop(0, n_first // chunk_a)
    def _(step):
        rows = pl.ds(pl.multiple_of(step * chunk_a, 16), chunk_a)
        window = p3_ref[rows, :]
        for parity in range(2):
            for tile in range(tiles):
                half = jnp.dot(
                    window,
                    w_in_ref[:, pl.ds(parity * HALF + tile * TILE, TILE)],
                    preferred_element_type=jnp.float32,
                )
                h1_ref[rows, pl.ds(parity * WIDE + 128 + tile * TILE, TILE)] = (
                    half + half * jnp.tanh(half)
                ).astype(jnp.bfloat16)

    seg = lax.broadcasted_iota(jnp.int32, (blk, 1), 0) % SEGS
    for b in range(5):
        head = pl.ds(b * blk, blk)
        h1_ref[head, :] = jnp.where(seg == 0, 0.0, h1_ref[head, :].astype(jnp.float32)).astype(
            jnp.bfloat16
        )
        tail = pl.ds((span + 5 + b) * blk, blk)
        h1_ref[tail, :] = jnp.where(
            seg == SEGS - 1, 0.0, h1_ref[tail, :].astype(jnp.float32)
        ).astype(jnp.bfloat16)

    @pl.loop(0, n_second // chunk_b)
    def _(step):
        base = pl.multiple_of(step * chunk_b, 16)
        total = jnp.zeros((chunk_b, 3 * OFFS), jnp.float32)
        for parity in range(2):
            for tile in range(tiles):
                half = jnp.zeros((chunk_b, TILE), jnp.float32)
                for tap in range(3):
                    half = half + jnp.dot(
                        h1_ref[
                            pl.ds(base + 4 * blk * tap, chunk_b),
                            pl.ds(parity * WIDE + tile * TILE, 512),
                        ],
                        w_mid_ref[tile % 3, pl.ds(tap * 512, 512), :],
                        preferred_element_type=jnp.float32,
                    )
                first = h1_ref[
                    pl.ds(base + 4 * blk, chunk_b),
                    pl.ds(parity * WIDE + 128 + tile * TILE, TILE),
                ].astype(jnp.float32)
                second = (first + (half + half * jnp.tanh(half))).astype(jnp.bfloat16)
                total = total + jnp.dot(
                    second,
                    w_out_ref[pl.ds(parity * HALF + tile * TILE, TILE), :],
                    preferred_element_type=jnp.float32,
                )
        z_ref[pl.ds(base, chunk_b), :] = total

    z_ref[pl.ds(0, blk), :] = jnp.where(seg == 0, 0.0, z_ref[pl.ds(0, blk), :])
    last = pl.ds((span + 1) * blk, blk)
    z_ref[last, :] = jnp.where(seg == SEGS - 1, 0.0, z_ref[last, :])

    n_out = span * blk

    @pl.loop(0, 8)
    def _(step):
        size = n_out // 8
        base = pl.multiple_of(step * size, 16)
        left = z_ref[pl.ds(base, size), :][:, 0:OFFS]
        mid = z_ref[pl.ds(base + blk, size), :][:, OFFS : 2 * OFFS]
        right = z_ref[pl.ds(base + 2 * blk, size), :][:, 2 * OFFS : 3 * OFFS]
        centre = p3_ref[pl.ds(base + 5 * blk, size), :].astype(jnp.float32)[:, OFFS : 2 * OFFS]
        out_ref[pl.ds(base, size), :] = (centre + (left + mid + right)).astype(jnp.bfloat16)


def largest_chunk(blocks, most):
    return max(d for d in range(1, most + 1) if blocks % d == 0)


def band_weights(conv_in, conv_mid, conv_out):
    half = jnp.bfloat16(0.5)
    offs = jnp.arange(OFFS)
    order = jnp.concatenate([offs[0::2], offs[1::2]])
    taps = jnp.arange(3)
    near = (order[:, None] - offs[None, :])[None]
    pick_in = (-near + 1 == taps[:, None, None]).astype(jnp.bfloat16)
    pick_out = (near + 1 == taps[:, None, None]).astype(jnp.bfloat16)
    w_in = jnp.einsum("alp,adc->dplc", pick_in, conv_in * half).reshape(3 * OFFS, OFFS * CHAN)
    w_out = jnp.einsum("alo,adc->lcdo", pick_out, conv_out).reshape(OFFS * CHAN, 3 * OFFS)
    scaled = conv_mid * half
    tiles = []
    for m in range(3):
        x = jnp.arange(512) + 256 * m - 128
        y = jnp.arange(256) + 256 * m
        rows = (x[:, None] % CHAN == jnp.arange(CHAN)[None]).astype(jnp.bfloat16)
        cols = (jnp.arange(CHAN)[:, None] == y[None] % CHAN).astype(jnp.bfloat16)
        tap = (x // CHAN)[:, None] - (y // CHAN)[None] + 1
        spread = jnp.einsum("xc,adce->adxe", rows, scaled)
        spread = jnp.einsum("adxe,ey->adxy", spread, cols)
        banded = jnp.where(tap[None] == 0, spread[0], jnp.bfloat16(0))
        banded = jnp.where(tap[None] == 1, spread[1], banded)
        banded = jnp.where(tap[None] == 2, spread[2], banded)
        tiles.append(banded.reshape(1536, 256))
    return w_in, jnp.stack(tiles), w_out


def filter_rows(panels, weights):
    bins, offs, samples = panels.shape
    span = samples // SEGS
    blk = bins * SEGS
    padded = jnp.pad(panels, ((0, 0), (0, 0), (6, 6)))
    segs = jnp.stack(
        [padded[:, :, s * span : s * span + span + 12] for s in range(SEGS)], axis=1
    )
    ext = segs.transpose(3, 0, 1, 2).reshape(span + 12, blk, offs)
    p3 = jnp.concatenate([ext[0 : span + 10], ext[1 : span + 11], ext[2 : span + 12]], axis=-1)
    p3 = p3.reshape((span + 10) * blk, 3 * offs)
    chunk_a = largest_chunk(span + 10, 40) * blk
    chunk_b = largest_chunk(span + 2, 44) * blk

    def body(*refs):
        kernel_body(span, chunk_a, chunk_b, *refs)

    return pl.pallas_call(
        body,
        out_shape=jax.ShapeDtypeStruct((span * blk, offs), jnp.bfloat16),
        in_specs=[pl.BlockSpec(memory_space=pltpu.VMEM)] * 4,
        out_specs=pl.BlockSpec(memory_space=pltpu.VMEM),
        scratch_shapes=[
            pltpu.VMEM(((span + 10) * blk, 2 * WIDE), jnp.bfloat16),
            pltpu.VMEM(((span + 2) * blk, 3 * offs), jnp.float32),
        ],
        compiler_params=pltpu.CompilerParams(vmem_limit_bytes=60 * 1024 * 1024),
        name="panel_filter",
    )(p3, *weights)


def local(predicted, observed, data_weight, bin_ids, offset_slots, conv_in, conv_mid, conv_out):
    tr_dev, samples = predicted.shape
    owners = lax.axis_size("bin")
    bin_dev = tr_dev // OFFS
    capacity = max(bin_dev, 2 * tr_dev // owners)
    slots = owners * capacity
    owner_dev = bin_ids // bin_dev
    local_bin = bin_ids % bin_dev
    row_index = jnp.arange(tr_dev, dtype=jnp.int32)
    earlier = row_index[None, :] < row_index[:, None]
    same_owner = owner_dev[:, None] == owner_dev[None, :]
    position = jnp.sum((same_owner & earlier).astype(jnp.int32), axis=1)
    send_slot = owner_dev * capacity + position
    panel_cell = local_bin * OFFS + offset_slots
    send_hit = jnp.arange(slots, dtype=jnp.int32)[:, None] == send_slot[None, :]
    send_pick = send_hit.astype(jnp.bfloat16)
    outgoing = jnp.dot(send_pick, predicted, preferred_element_type=jnp.float32)
    outgoing = outgoing.astype(jnp.bfloat16).reshape(owners, capacity, samples)
    outgoing_cells = (
        jnp.sum(jnp.where(send_hit, panel_cell[None, :] + 1, 0), axis=1) - 1
    ).reshape(owners, capacity)
    arrived_cells = lax.all_to_all(
        outgoing_cells, "bin", split_axis=0, concat_axis=0, tiled=True
    )
    arrived = lax.all_to_all(outgoing, "bin", split_axis=0, concat_axis=0, tiled=True)
    weights = band_weights(conv_in, conv_mid, conv_out)
    cells = jnp.arange(tr_dev, dtype=jnp.int32)
    cell_pick = (arrived_cells.reshape(-1)[:, None] == cells[None, :]).astype(jnp.bfloat16)
    panels = jnp.einsum(
        "sc,st->ct", cell_pick, arrived.reshape(slots, samples), preferred_element_type=jnp.float32
    )
    panels = panels.astype(jnp.bfloat16).reshape(bin_dev, OFFS, samples)
    rows = filter_rows(panels, weights).reshape(samples // SEGS, bin_dev, SEGS, OFFS)
    filtered = rows.transpose(1, 3, 2, 0).reshape(tr_dev, samples)
    answer = jnp.dot(cell_pick, filtered, preferred_element_type=jnp.float32)
    answer = answer.astype(jnp.bfloat16).reshape(owners, capacity, samples)
    returned = lax.all_to_all(answer, "bin", split_axis=0, concat_axis=0, tiled=True)
    own_rows = jnp.einsum(
        "sr,st->rt",
        send_pick,
        returned.reshape(slots, samples),
        preferred_element_type=jnp.float32,
    )
    misfit = data_weight * (own_rows - observed)
    misfit_total = lax.psum(jnp.sum(misfit * misfit), "bin")
    mean_square = misfit_total / (tr_dev * owners * samples)
    return (misfit * lax.rsqrt(mean_square + 1e-05)).astype(jnp.bfloat16)


def solution(mesh):
    in_specs = (
        P(("line", "bin"), None),
        P(("line", "bin"), None),
        P(("line", "bin"), None),
        P(("line", "bin")),
        P(("line", "bin")),
        P(),
        P(),
        P(),
    )
    out_specs = P(("line", "bin"), None)
    return jax.shard_map(local, mesh=mesh, in_specs=in_specs, out_specs=out_specs, check_vma=False)
```

time: 753 us -> 234 us (0.31)
  matrix products: 526 us -> 13.2 us
  Pallas kernels: 0 us -> 67.4 us
  other arithmetic: 71 us -> 17.9 us
  waiting for transfers between devices: 45.7 us -> 14.8 us
  blocking collectives: 35.5 us -> 65.2 us
  loops' own time: 24 us -> 0 us
  local copies, waits for them, and re-layouts: 27.4 us -> 40 us
    dot_general x90 -> x9, matrix products: 526 us -> 13.2 us  [the longest x3 4.61 us: band_weights(): spread = jnp.einsum('adxe,ey->adxy', spread, cols)]
    pallas_call x0 -> x1, Pallas kernels: none -> 67.4 us  [filter_rows(): pl.pallas_call(body, out_shape=jax.ShapeDtypeStruct((span * blk, offs), j...]
    convert_element_type x20 -> x0, other arithmetic: 62.2 us -> none  [the longest x5 50.5 us: one_block(): jnp.where(inside, jax.nn.silu(first_sum), 0.0).astype(jnp.bfloat16)]
    all_to_all x0 -> x1, blocking collectives: none -> 31.5 us  [local(): lax.all_to_all(answer, 'bin', split_axis=0, concat_axis=0, tiled=True)]
    another operation x1 -> x0, loops' own time: 24 us -> none  [filter_panels(): result = lax.fori_loop(0, blocks, one_block, result)]
    all_to_all x1 -> x0, waiting for transfers between devices: 22.9 us -> none  [local(): lax.all_to_all(answer, 'bin', split_axis=0, concat_axis=0, tiled=True)]
    reshape x1 -> x4, local copies, waits for them, and re-layouts: 0.08 us -> 19.8 us  [the longest x2 10.1 us: band_weights(): jnp.einsum('alo,adc->lcdo', pick_out, conv_out)]
    dynamic_update_slice x5 -> x0, local copies, waits for them, and re-layouts: 10.5 us -> none  [one_block(): return lax.dynamic_update_slice_in_dim(result, piece, start, 2)]
  transfers between devices with their start and end apart: 3 -> 2, of which waited for: 3 -> 1; matrix products, arithmetic and copies ran while one was open for 1% -> 21% of each run, Pallas kernels for 0% -> 0%
where the time goes in v1:
time: 234 us; the launch traced here: 233 us
  Pallas kernels  67.4 us (29%)
  blocking collectives  65.2 us (28%)
  local copies, waits for them, and re-layouts  40 us (17%)
  other arithmetic  17.9 us (8%)
  waiting for transfers between devices  14.8 us (6%)
  starting transfers between devices  13.4 us (6%)
  matrix products  13.2 us (6%)
    pallas_call x1, Pallas kernels, filter_rows(): pl.pallas_call(body, out_shape=jax.ShapeDtypeStruct((span * blk, offs), j...  67.4 us
    psum x1, blocking collectives, local(): misfit_total = lax.psum(jnp.sum(misfit * misfit), 'bin')  33.6 us
    all_to_all x1, blocking collectives, local(): lax.all_to_all(answer, 'bin', split_axis=0, concat_axis=0, tiled=True)  31.5 us
    all_to_all x1, waiting for transfers between devices, local(): lax.all_to_all(outgoing, 'bin', split_axis=0, concat_axis=0, tiled=True)  14.8 us
    reshape x2, local copies, waits for them, and re-layouts, band_weights(): jnp.einsum('alo,adc->lcdo', pick_out, conv_out)  10.1 us
    all_to_all x1, starting transfers between devices, local(): lax.all_to_all(outgoing_cells, 'bin', split_axis=0, concat_axis=0, tiled=...  7.41 us
    reshape x1, local copies, waits for them, and re-layouts, band_weights(): jnp.einsum('alp,adc->dplc', pick_in, conv_in * half)  7.35 us
    all_to_all x1, starting transfers between devices, local(): lax.all_to_all(outgoing, 'bin', split_axis=0, concat_axis=0, tiled=True)  6.03 us
  transfers between devices with their start and end apart: 2, of which 1 were waited for; matrix products, arithmetic and copies ran while one was open for 21% of the time, Pallas kernels for 0%

profile of v1, /device:TPU:0, one launch (start us, length us, event | category | flops | bytes accessed | tf_op | source)
XLA Modules:
  0.0 233.0 jit_solution(17246871893971104513)
XLA Ops:
  1.8 7.4 %all-to-all-start = ((s32[16,1,16]{2,1,0:T(1,128)}), s32[16,1,16]{2,1,0:T(1,128)}, u32[]{:S(2)}, u32[]{:S(2)}) async-start(s32[16,1,16]{2,1,0:T(1,128)} %sub.225), calls=%async_computation | async-start | bytes 16384 | tf_op jit(solution)/shard_map/all_to_all | solution.py:182
  12.8 1.5 convolution_convert_fusion.1
  14.3 1.9 fusion.2
  16.2 1.5 fusion.105
  17.7 1.0 fusion.1
  18.8 1.5 fusion.106
  21.3 1.0 fusion.4
  22.3 1.6 fusion.7
  23.9 1.7 fusion.3
  25.6 1.6 convolution_bitcast_fusion
  27.2 2.3 convolution_bitcast_fusion.1
  29.5 1.1 fusion.10
  30.6 3.3 %copy.55 = bf16[64,48,3,64]{3,2,1,0:T(4,128)(2,1)} copy(bf16[64,48,3,64]{3,1,2,0:T(8,128)(2,1)S(1)} %convolution_bitcast_fusion) | data formatting | bytes 2359296 | tf_op jit(solution)/shard_map/reshape | solution.py:112
  33.9 6.7 %reshape.692.refs_3_ = bf16[3072,192]{1,0:T(8,128)(2,1)} reshape(bf16[64,48,3,64]{3,2,1,0:T(4,128)(2,1)} %copy.55) | data formatting | bytes 2359296 | tf_op jit(solution)/shard_map/reshape | solution.py:112
  40.7 5.2 %copy.34 = bf16[3,64,64,48]{3,2,1,0:T(8,128)(2,1)} copy(bf16[3,64,64,48]{1,3,2,0:T(8,128)(2,1)} %convolution_bitcast_fusion.1) | data formatting | bytes 2359296 | tf_op jit(solution)/shard_map/alp,adc->dplc/transpose | solution.py:111
  45.9 7.3 %reshape.676.refs_1_ = bf16[192,3072]{1,0:T(8,128)(2,1)} reshape(bf16[3,64,64,48]{3,2,1,0:T(8,128)(2,1)} %copy.34) | data formatting | bytes 2359296 | tf_op jit(solution)/shard_map/reshape | solution.py:111
  53.2 6.0 %all-to-all-start.1 = ((bf16[16,16,2048]{2,1,0:T(8,128)(2,1)}), bf16[16,16,2048]{2,1,0:T(8,128)(2,1)}, u32[]{:S(2)}, u32[]{:S(2)}) async-start(bf16[16,16,2048]{2,1,0:T(8,128)(2,1)} %bitcast.181), calls=%async_computation.1 | async-start | bytes 2097152 | tf_op jit(solution)/shard_map/all_to_all | solution.py:185
  63.8 1.7 pad_maximum_fusion.refs_2_
  66.0 1.4 reduce.3
  67.4 14.8 %all-to-all-done.1 = bf16[16,16,2048]{2,1,0:T(8,128)(2,1)} async-done(((bf16[16,16,2048]{2,1,0:T(8,128)(2,1)}), bf16[16,16,2048]{2,1,0:T(8,128)(2,1)}, u32[]{:S(2)}, u32[]{:S(2)}) %all-to-all-start.1) | async-done | bytes 1048608 | tf_op jit(solution)/shard_map/all_to_all | solution.py:185
  82.3 1.6 convolution_convert_fusion.2
  84.8 1.5 fusion.107
  86.3 1.0 copy.30
  87.3 2.0 copy.31
  89.3 1.8 copy.32
  91.1 3.7 %pad_maximum_fusion.1.refs_0_ = bf16[4256,192]{1,0:T(8,128)(2,1)} fusion(bf16[4256,64]{1,0:T(8,128)(2,1)} %bitcast.179, bf16[4256,64]{1,0:T(8,128)(2,1)S(1)} %bitcast.178, bf16[4256,64]{1,0:T(8,128)(2,1)S(1)} %bitcast.177), kind=kLoop, calls=%fused_computation.6 | loop fusion | flops 4902912 | bytes 3268608 | tf_op jit(solution)/shard_map/concatenate | solution.py:139
  94.7 67.4 %panel_filter.1 = bf16[4096,64]{1,0:T(8,128)(2,1)} custom-call(bf16[4256,192]{1,0:T(8,128)(2,1)} %pad_maximum_fusion.1.refs_0_, bf16[192,3072]{1,0:T(8,128)(2,1)} %reshape.676.refs_1_, bf16[3,1536,256]{2,1,0:T(8,128)(2,1)} %pad_maximum_fusion.refs_2_, bf16[3072,192]{1,0:T(8,128)(2,1)} %reshape.692.refs_3_), custom_call_target="tpu_custom_call" | custom-call | tf_op jit(solution)/shard_map/panel_filter/pallas_call | solution.py:147
  162.1 2.4 %copy.41 = bf16[256,2,8,64]{0,2,3,1:T(8,128)(2,1)S(1)} copy(bf16[256,2,8,64]{3,2,1,0:T(8,128)(2,1)} %bitcast.183) | data formatting | bytes 1048576 | tf_op jit(solution)/shard_map/reshape | solution.py:193
  165.2 31.5 %all_to_all.16 = bf16[16,16,2048]{2,1,0:T(8,128)(2,1)S(1)} all-to-all(bf16[16,16,2048]{2,1,0:T(8,128)(2,1)S(1)} %bitcast.182), channel_id=1, replica_groups=mesh['line'=2,'bin'=16] {'bin'}, dimensions={0} | all-to-all | bytes 2097152 | tf_op jit(solution)/shard_map/all_to_all | solution.py:197
  196.7 1.1 multiply_reduce_fusion
  197.8 33.6 %psum.7 = f32[]{:T(128)} all-reduce(f32[]{:T(128)} %get-tuple-element.30), channel_id=1, replica_groups=mesh['line'=2,'bin'=16] {'bin'}, use_global_device_ids=true, to_apply=%region_3.4 | all-reduce | flops 1 | bytes 8 | tf_op jit(solution)/shard_map/psum | solution.py:205
  232.1 0.9 multiply_convert_fusion
  (90 shorter events, 12.8 us)
Async XLA Ops:
  0.0 12.8 %copy-start = (bf16[128,2048]{1,0:T(8,128)(2,1)S(1)}, bf16[128,2048]{1,0:T(8,128)(2,1)}, u32[]{:S(2)}) copy-start(bf16[128,2048]{1,0:T(8,128)(2,1)} %param.8) | copy-start | bytes 1572868
  0.9 13.4 %copy-start.16 = (s32[128]{0:T(128)}, s32[128]{0:T(128)S(1)}, u32[]{:S(2)}) copy-start(s32[128]{0:T(128)S(1)} %multiply_add_fusion) | copy-start | bytes 1540
  1.8 51.5 %all-to-all-start = ((s32[16,1,16]{2,1,0:T(1,128)}), s32[16,1,16]{2,1,0:T(1,128)}, u32[]{:S(2)}, u32[]{:S(2)}) async-start(s32[16,1,16]{2,1,0:T(1,128)} %sub.225), calls=%async_computation | async-start | bytes 16384 | tf_op jit(solution)/shard_map/all_to_all | solution.py:182
  16.2 1.5 copy-start.9
  18.7 2.6 %copy-start.18 = (bf16[3,3,48]{2,1,0:T(4,128)(2,1)S(1)}, bf16[3,3,48]{2,1,0:T(4,128)(2,1)}, u32[]{:S(2)}) copy-start(bf16[3,3,48]{2,1,0:T(4,128)(2,1)} %param.13) | copy-start | bytes 2596
  25.6 3.9 %copy-start.15 = (s32[512]{0:T(512)S(1)}, s32[512]{0:T(512)}, u32[]{:S(2)}) copy-start(s32[512]{0:T(512)} %add_select_fusion.5) | copy-start | bytes 6148
  25.6 3.9 %copy-start.19 = (s32[256]{0:T(256)S(1)}, s32[256]{0:T(256)}, u32[]{:S(2)}) copy-start(s32[256]{0:T(256)} %and_select_fusion.5) | copy-start | bytes 3076
  53.2 29.0 %all-to-all-start.1 = ((bf16[16,16,2048]{2,1,0:T(8,128)(2,1)}), bf16[16,16,2048]{2,1,0:T(8,128)(2,1)}, u32[]{:S(2)}, u32[]{:S(2)}) async-start(bf16[16,16,2048]{2,1,0:T(8,128)(2,1)} %bitcast.181), calls=%async_computation.1 | async-start | bytes 2097152 | tf_op jit(solution)/shard_map/all_to_all | solution.py:185
  59.3 0.9 copy-start.14
  59.3 1.0 copy-start.13
  59.3 1.1 copy-start.12
  60.4 0.9 copy-start.11
  60.5 1.1 copy-start.10
  60.5 1.4 copy-start.5
  60.6 1.4 copy-start.6
  61.0 1.3 copy-start.1
  61.0 1.6 copy-start.2
  61.0 1.8 copy-start.3
  61.0 2.0 copy-start.4
  164.6 32.1 %copy-start.7 = (f32[128,2048]{1,0:T(8,128)S(1)}, f32[128,2048]{1,0:T(8,128)}, u32[]{:S(2)}) copy-start(f32[128,2048]{1,0:T(8,128)} %param.10) | copy-start | bytes 3145732
  164.6 32.1 %copy-start.8 = (f32[128,2048]{1,0:T(8,128)S(1)}, f32[128,2048]{1,0:T(8,128)}, u32[]{:S(2)}) copy-start(f32[128,2048]{1,0:T(8,128)} %param.9) | copy-start | bytes 3145732
  164.6 32.1 %copy-start.17 = (s32[128]{0:T(128)S(1)}, s32[128]{0:T(128)}, u32[]{:S(2)}) copy-start(s32[128]{0:T(128)} %copy-done.16) | copy-start | bytes 1540

commit v2 on v1

v2 whole, which is shorter than its diff:
```python
import jax
import jax.numpy as jnp
from jax import lax
from jax.experimental import pallas as pl
from jax.experimental.pallas import tpu as pltpu
from jax.sharding import PartitionSpec as P

OFFS = 64
CHAN = 48
SEGS = 16
MOST = 46
HALF = (OFFS // 2) * CHAN
WIDE = HALF + 256
TILE = 256


def kernel_body(
    span,
    chunk_a,
    chunk_b,
    ext_ref,
    w_in_ref,
    w_mid0_ref,
    w_mid1_ref,
    w_mid2_ref,
    w_out_ref,
    out_ref,
    p3_ref,
    h1_ref,
    z_ref,
):
    w_mid_refs = (w_mid0_ref, w_mid1_ref, w_mid2_ref)
    blk = SEGS
    n_first = (span + 10) * blk
    n_second = (span + 2) * blk
    tiles = HALF // TILE
    zero_cols = jnp.zeros((n_first, 128), jnp.bfloat16)
    for tap in range(3):
        p3_ref[:, pl.ds(tap * OFFS, OFFS)] = ext_ref[pl.ds(tap * blk, n_first), :]
    for parity in range(2):
        h1_ref[:, pl.ds(parity * WIDE, 128)] = zero_cols
        h1_ref[:, pl.ds(parity * WIDE + 128 + HALF, 128)] = zero_cols

    @pl.loop(0, n_first // chunk_a)
    def _(step):
        rows = pl.ds(pl.multiple_of(step * chunk_a, 16), chunk_a)
        window = p3_ref[rows, :]
        for parity in range(2):
            for tile in range(tiles):
                half = jnp.dot(
                    window,
                    w_in_ref[:, pl.ds(parity * HALF + tile * TILE, TILE)],
                    preferred_element_type=jnp.float32,
                )
                h1_ref[rows, pl.ds(parity * WIDE + 128 + tile * TILE, TILE)] = (
                    half + half * jnp.tanh(half)
                ).astype(jnp.bfloat16)

    seg = lax.broadcasted_iota(jnp.int32, (blk, 1), 0)
    for b in range(5):
        head = pl.ds(b * blk, blk)
        h1_ref[head, :] = jnp.where(seg == 0, 0.0, h1_ref[head, :].astype(jnp.float32)).astype(
            jnp.bfloat16
        )
        tail = pl.ds((span + 5 + b) * blk, blk)
        h1_ref[tail, :] = jnp.where(
            seg == SEGS - 1, 0.0, h1_ref[tail, :].astype(jnp.float32)
        ).astype(jnp.bfloat16)

    @pl.loop(0, n_second // chunk_b)
    def _(step):
        base = pl.multiple_of(step * chunk_b, 16)
        total = jnp.zeros((chunk_b, 3 * OFFS), jnp.float32)
        for parity in range(2):
            for tile in range(tiles):
                half = jnp.zeros((chunk_b, TILE), jnp.float32)
                for tap in range(3):
                    half = half + jnp.dot(
                        h1_ref[
                            pl.ds(base + 4 * blk * tap, chunk_b),
                            pl.ds(parity * WIDE + tile * TILE, 512),
                        ],
                        w_mid_refs[tile % 3][pl.ds(tap * 512, 512), :],
                        preferred_element_type=jnp.float32,
                    )
                first = h1_ref[
                    pl.ds(base + 4 * blk, chunk_b),
                    pl.ds(parity * WIDE + 128 + tile * TILE, TILE),
                ].astype(jnp.float32)
                second = (first + (half + half * jnp.tanh(half))).astype(jnp.bfloat16)
                total = total + jnp.dot(
                    second,
                    w_out_ref[pl.ds(parity * HALF + tile * TILE, TILE), :],
                    preferred_element_type=jnp.float32,
                )
        z_ref[pl.ds(base, chunk_b), :] = total

    z_ref[pl.ds(0, blk), :] = jnp.where(seg == 0, 0.0, z_ref[pl.ds(0, blk), :])
    last = pl.ds((span + 1) * blk, blk)
    z_ref[last, :] = jnp.where(seg == SEGS - 1, 0.0, z_ref[last, :])

    n_out = span * blk

    @pl.loop(0, 8)
    def _(step):
        size = n_out // 8
        base = pl.multiple_of(step * size, 16)
        left = z_ref[pl.ds(base, size), :][:, 0:OFFS]
        mid = z_ref[pl.ds(base + blk, size), :][:, OFFS : 2 * OFFS]
        right = z_ref[pl.ds(base + 2 * blk, size), :][:, 2 * OFFS : 3 * OFFS]
        centre = p3_ref[pl.ds(base + 5 * blk, size), :].astype(jnp.float32)[:, OFFS : 2 * OFFS]
        out_ref[pl.ds(base, size), :] = (centre + (left + mid + right)).astype(jnp.bfloat16)


def largest_chunk(blocks, most):
    return max(d for d in range(1, most + 1) if blocks % d == 0)


def band_weights(conv_in, conv_mid, conv_out):
    lane = jnp.arange(OFFS * CHAN)
    place = lane // CHAN
    offset = 2 * (place % (OFFS // 2)) + place // (OFFS // 2)
    spread = (jnp.arange(CHAN)[:, None] == (lane % CHAN)[None]).astype(jnp.bfloat16)
    zero = jnp.bfloat16(0)
    half = jnp.bfloat16(0.5)
    others = jnp.arange(OFFS)

    near = others[:, None] - offset[None, :] + 1
    wide_in = jnp.dot((conv_in * half).reshape(9, CHAN), spread).reshape(3, 3, 1, OFFS * CHAN)
    w_in = zero
    for a in range(3):
        w_in = jnp.where((near == a)[None], wide_in[a], w_in)
    w_in = w_in.reshape(3 * OFFS, OFFS * CHAN)

    near = offset[:, None] - jnp.tile(others, 3)[None, :] + 1
    w_out = zero
    for a in range(3):
        w_out = jnp.where(
            near == a, jnp.dot(spread.T, jnp.repeat(conv_out[a].T, OFFS, axis=1)), w_out
        )

    scaled = conv_mid * half
    tiles = []
    for m in range(3):
        x = jnp.arange(512) + 256 * m - 128
        y = jnp.arange(256) + 256 * m
        rows = (x[:, None] % CHAN == jnp.arange(CHAN)[None]).astype(jnp.bfloat16)
        cols = (jnp.arange(CHAN)[:, None] == y[None] % CHAN).astype(jnp.bfloat16)
        tap = (x // CHAN)[:, None] - (y // CHAN)[None] + 1
        wide = jnp.einsum("adce,ey->adcy", scaled, cols)
        wide = jnp.einsum("xc,adcy->adxy", rows, wide)
        banded = jnp.where(tap[None] == 0, wide[0], zero)
        banded = jnp.where(tap[None] == 1, wide[1], banded)
        banded = jnp.where(tap[None] == 2, wide[2], banded)
        tiles.append(banded.reshape(1536, 256))
    return w_in, tiles[0], tiles[1], tiles[2], w_out


def filter_rows(panel, weights):
    samples, offs = panel.shape
    span = samples // SEGS
    blk = SEGS
    segs = panel.reshape(SEGS, span, offs)
    none = jnp.zeros((1, 6, offs), panel.dtype)
    before = jnp.concatenate([none, segs[:-1, span - 6 :]])
    after = jnp.concatenate([segs[1:, :6], none])
    ext = jnp.concatenate([before, segs, after], axis=1).transpose(1, 0, 2)
    ext = ext.reshape((span + 12) * blk, offs)
    chunk_a = largest_chunk(span + 10, MOST) * blk
    chunk_b = largest_chunk(span + 2, MOST) * blk

    def body(*refs):
        kernel_body(span, chunk_a, chunk_b, *refs)

    rows = pl.pallas_call(
        body,
        out_shape=jax.ShapeDtypeStruct((span * blk, offs), jnp.bfloat16),
        in_specs=[pl.BlockSpec(memory_space=pltpu.VMEM)] * 6,
        out_specs=pl.BlockSpec(memory_space=pltpu.VMEM),
        scratch_shapes=[
            pltpu.VMEM(((span + 10) * blk, 3 * offs), jnp.bfloat16),
            pltpu.VMEM(((span + 10) * blk, 2 * WIDE), jnp.bfloat16),
            pltpu.VMEM(((span + 2) * blk, 3 * offs), jnp.float32),
        ],
        compiler_params=pltpu.CompilerParams(vmem_limit_bytes=48 * 1024 * 1024),
        name="panel_filter",
    )(ext, *weights)
    return rows.reshape(span, SEGS, offs).transpose(1, 0, 2).reshape(samples, offs)


def local(predicted, observed, data_weight, bin_ids, offset_slots, conv_in, conv_mid, conv_out):
    tr_dev, samples = predicted.shape
    owners = lax.axis_size("bin")
    bin_dev = tr_dev // OFFS
    capacity = max(1, tr_dev // owners)
    slots = owners * capacity
    row_index = jnp.arange(tr_dev, dtype=jnp.int32)
    earlier = row_index[None, :] < row_index[:, None]
    same_bin = bin_ids[:, None] == bin_ids[None, :]
    position = jnp.sum((same_bin & earlier).astype(jnp.int32), axis=1)
    owner_slot = (bin_ids // bin_dev) * capacity + position
    local_bin = bin_ids % bin_dev
    mark = jnp.broadcast_to((offset_slots + 1).astype(jnp.bfloat16)[:, None], (tr_dev, 128))
    labelled = jnp.concatenate([predicted, mark], axis=1)
    slot_index = jnp.arange(slots, dtype=jnp.int32)
    offsets = jnp.arange(OFFS, dtype=jnp.int32)

    picks = []
    arrivals = []
    for b in range(bin_dev):
        send_slot = jnp.where(local_bin == b, owner_slot, -1)
        pick = (slot_index[:, None] == send_slot[None, :]).astype(jnp.bfloat16)
        outgoing = jnp.dot(pick, labelled, preferred_element_type=jnp.float32)
        outgoing = outgoing.astype(jnp.bfloat16).reshape(owners, capacity, samples + 128)
        arrived = lax.all_to_all(outgoing, "bin", split_axis=0, concat_axis=0, tiled=True)
        picks.append(pick)
        arrivals.append(arrived.reshape(slots, samples + 128))

    weights = band_weights(conv_in, conv_mid, conv_out)
    own_rows = 0.0
    for b in range(bin_dev):
        cell = arrivals[b][:, samples].astype(jnp.int32) - 1
        cell_pick = (cell[:, None] == offsets[None, :]).astype(jnp.bfloat16)
        panel = jnp.einsum(
            "sc,st->tc",
            cell_pick,
            arrivals[b][:, :samples],
            preferred_element_type=jnp.float32,
        ).astype(jnp.bfloat16)
        filtered = filter_rows(panel, weights)
        answer = jnp.einsum("sc,tc->st", cell_pick, filtered, preferred_element_type=jnp.float32)
        answer = answer.astype(jnp.bfloat16).reshape(owners, capacity, samples)
        returned = lax.all_to_all(answer, "bin", split_axis=0, concat_axis=0, tiled=True)
        own_rows = own_rows + jnp.einsum(
            "sr,st->rt",
            picks[b],
            returned.reshape(slots, samples),
            preferred_element_type=jnp.float32,
        )
    misfit = data_weight * (own_rows - observed)
    share = jnp.broadcast_to(jnp.sum(misfit * misfit), (owners, 1, 128))
    shares = lax.all_to_all(share, "bin", split_axis=0, concat_axis=0, tiled=True)
    misfit_total = jnp.sum(shares[:, 0, 0])
    mean_square = misfit_total / (tr_dev * owners * samples)
    return (misfit * lax.rsqrt(mean_square + 1e-05)).astype(jnp.bfloat16)


def solution(mesh):
    in_specs = (
        P(("line", "bin"), None),
        P(("line", "bin"), None),
        P(("line", "bin"), None),
        P(("line", "bin")),
        P(("line", "bin")),
        P(),
        P(),
        P(),
    )
    out_specs = P(("line", "bin"), None)
    return jax.shard_map(local, mesh=mesh, in_specs=in_specs, out_specs=out_specs, check_vma=False)
```

time: 234 us -> 207 us (0.88)
  blocking collectives: 65.2 us -> 10.3 us
  matrix products: 13.2 us -> 27.8 us
  starting transfers between devices: 13.4 us -> 25.5 us
  other arithmetic: 17.9 us -> 22.1 us
  local copies, waits for them, and re-layouts: 40 us -> 37.6 us
    psum x1 -> x0, blocking collectives: 33.6 us -> none  [local(): misfit_total = lax.psum(jnp.sum(misfit * misfit), 'bin')]
    all_to_all x1, blocking collectives: 31.5 us -> 10.3 us  [local(): lax.all_to_all(share, 'bin', split_axis=0, concat_axis=0, tiled=True)]
    all_to_all x1 -> x2, waiting for transfers between devices: 14.8 us -> 0.01 us  [local(): lax.all_to_all(outgoing, 'bin', split_axis=0, concat_axis=0, tiled=True)]
    dot_general x9 -> x15, matrix products: 13.2 us -> 27.8 us  [the longest x3 9.03 us: band_weights(): jnp.dot(spread.T, jnp.repeat(conv_out[a].T, OFFS, axis=1))]
    all_to_all x1 -> x2, waiting for transfers between devices: 0.01 us -> 13.1 us  [local(): lax.all_to_all(answer, 'bin', split_axis=0, concat_axis=0, tiled=True)]
    reshape x4 -> x8, local copies, waits for them, and re-layouts: 19.8 us -> 9.42 us  [the longest x2 4.58 us: filter_rows(): segs = panel.reshape(SEGS, span, offs)]
    slice x9 -> x15, local copies, waits for them, and re-layouts: 9.68 us -> 19.6 us  [the longest x6 7.91 us: band_weights(): banded = jnp.where(tap[None] == 2, wide[2], banded)]
    all_to_all x1 -> x2, starting transfers between devices: 6.03 us -> 13.6 us  [local(): lax.all_to_all(outgoing, 'bin', split_axis=0, concat_axis=0, tiled=True)]
  transfers between devices with their start and end apart: 2 -> 4, of which waited for: 1 -> 1; matrix products, arithmetic and copies ran while one was open for 21% -> 35% of each run, Pallas kernels for 0% -> 33%
where the time goes in v2:
time: 207 us; the launch traced here: 205 us
  Pallas kernels  67.7 us (33%)
  local copies, waits for them, and re-layouts  37.6 us (18%)
  matrix products  27.8 us (13%)
  starting transfers between devices  25.5 us (12%)
  other arithmetic  22.1 us (11%)
  waiting for transfers between devices  13.1 us (6%)
  blocking collectives  10.3 us (5%)
    pallas_call x2, Pallas kernels, filter_rows(): pl.pallas_call(body, out_shape=jax.ShapeDtypeStruct((span * blk, offs), j...  67.7 us
    all_to_all x2, starting transfers between devices, local(): lax.all_to_all(outgoing, 'bin', split_axis=0, concat_axis=0, tiled=True)  13.6 us
    all_to_all x2, waiting for transfers between devices, local(): lax.all_to_all(answer, 'bin', split_axis=0, concat_axis=0, tiled=True)  13.1 us
    all_to_all x2, starting transfers between devices, local(): lax.all_to_all(answer, 'bin', split_axis=0, concat_axis=0, tiled=True)  12 us
    all_to_all x1, blocking collectives, local(): lax.all_to_all(share, 'bin', split_axis=0, concat_axis=0, tiled=True)  10.3 us
    dot_general x3, matrix products, band_weights(): jnp.dot(spread.T, jnp.repeat(conv_out[a].T, OFFS, axis=1))  9.03 us
    slice x6, local copies, waits for them, and re-layouts, band_weights(): banded = jnp.where(tap[None] == 2, wide[2], banded)  7.91 us
    unnamed x80, local copies, waits for them, and re-layouts  6.53 us
  transfers between devices with their start and end apart: 4, of which 1 were waited for; matrix products, arithmetic and copies ran while one was open for 35% of the time, Pallas kernels for 33%

profile of v2, /device:TPU:0, one launch (start us, length us, event | category | flops | bytes accessed | tf_op | source)
XLA Modules:
  0.0 205.1 jit_solution(15799718308177730450)
XLA Ops:
  2.9 2.2 %fusion = bf16[16,8,2176]{2,1,0:T(8,128)(2,1)} fusion(bf16[128,128]{1,0:T(8,128)(2,1)S(1)} %broadcast_in_dim.193, bf16[128,2048]{1,0:T(8,128)(2,1)} %param.8, s32[128]{0:T(128)S(1)} %compare_select_fusion.1), kind=kOutput, calls=%fused_computation.5 | convolution fusion | flops 72712192 | bytes 1114624 | tf_op jit(solution)/shard_map/dot_general | solution.py:213
  5.1 7.4 %all-to-all-start = ((bf16[16,8,2176]{2,1,0:T(8,128)(2,1)}), bf16[16,8,2176]{2,1,0:T(8,128)(2,1)}, u32[]{:S(2)}, u32[]{:S(2)}) async-start(bf16[16,8,2176]{2,1,0:T(8,128)(2,1)} %fusion), calls=%async_computation | async-start | bytes 1114112 | tf_op jit(solution)/shard_map/all_to_all | solution.py:215
  19.6 1.4 fusion.140
  20.9 1.6 convolution_bitcast_fusion
  22.6 1.5 fusion.138
  24.1 1.6 convolution_bitcast_fusion.1
  25.7 1.5 fusion.139
  28.2 2.1 %fusion.1 = bf16[16,8,2176]{2,1,0:T(8,128)(2,1)} fusion(bf16[128,128]{1,0:T(8,128)(2,1)S(1)} %broadcast_in_dim.193, bf16[128,2048]{1,0:T(8,128)(2,1)} %param.8, s32[128]{0:T(128)S(1)} %copy-done.28), kind=kOutput, calls=%fused_computation.6 | convolution fusion | flops 72712192 | bytes 1114624 | tf_op jit(solution)/shard_map/dot_general | solution.py:213
  30.3 1.8 fusion.42
  33.2 2.6 %convolution_select_fusion = bf16[3072,192]{1,0:T(8,128)(2,1)} fusion(bf16[48,192]{1,0:T(8,128)(2,1)S(1)} %reshape.666, s32[192]{0:T(256)S(1)} %sub.327, s32[3072]{0:T(1024)S(1)} %get-tuple-element.42, s32[3072]{0:T(1024)S(1)} %copy-done.25), kind=kOutput, calls=%fused_computation | convolution fusion | flops 59129856 | bytes 1223424 | tf_op jit(solution)/shard_map/dot_general | solution.py:139
  36.1 3.8 %convolution_select_fusion.1 = bf16[3072,192]{1,0:T(8,128)(2,1)} fusion(bf16[3072,192]{1,0:T(8,128)(2,1)} %convolution_select_fusion, bf16[48,192]{1,0:T(8,128)(2,1)S(1)} %reshape.665, s32[192]{0:T(256)S(1)} %sub.327, s32[3072]{0:T(1024)S(1)} %get-tuple-element.42, s32[3072]{0:T(1024)S(1)} %copy-done.25), kind=kOutput, calls=%fused_computation.1 | convolution fusion | flops 59129856 | bytes 2403072 | tf_op jit(solution)/shard_map/dot_general | solution.py:139
  40.5 6.2 %all-to-all-start.2 = ((bf16[16,8,2176]{2,1,0:T(8,128)(2,1)}), bf16[16,8,2176]{2,1,0:T(8,128)(2,1)}, u32[]{:S(2)}, u32[]{:S(2)}) async-start(bf16[16,8,2176]{2,1,0:T(8,128)(2,1)} %fusion.1), calls=%async_computation.2 | async-start | bytes 1114112 | tf_op jit(solution)/shard_map/all_to_all | solution.py:215
  47.7 2.4 %copy.106 = bf16[1,3,512,256]{3,2,1,0:T(8,128)(2,1)} copy(bf16[1,3,512,256]{2,3,1,0:T(8,128)(2,1)} %get-tuple-element.15) | data formatting | bytes 1572864 | tf_op jit(solution)/shard_map/slice | solution.py:152
  52.4 2.5 %copy.112 = bf16[1,3,512,256]{3,2,1,0:T(8,128)(2,1)} copy(bf16[1,3,512,256]{2,3,1,0:T(8,128)(2,1)} %get-tuple-element.9) | data formatting | bytes 1572864 | tf_op jit(solution)/shard_map/slice | solution.py:152
  61.7 1.7 bitcast_select_fusion.8.refs_2_
  64.0 2.5 %bitcast_select_fusion.2 = (bf16[1536,256]{1,0:T(8,128)(2,1)S(1)}, bf16[1536,256]{1,0:T(8,128)(2,1)S(1)}) fusion(bf16[1,3,512,256]{3,2,1,0:T(8,128)(2,1)S(1)} %copy-done.10, bf16[1,3,512,256]{3,2,1,0:T(8,128)(2,1)S(1)} %copy-done.11, bf16[1,3,512,256]{3,2,1,0:T(8,128)(2,1)S(1)} %copy-done.12, pred[512,256]{1,0:T(8,128)(4,1)S(1)} %copy-done.20, ...), kind=kLoop, calls=%fused_computation.25 | loop fusion | flops 2359296 | bytes 7077888 | tf_op jit(solution)/shard_map/jit(_where)/select_n | solution.py:154
  66.5 2.6 %convolution_select_fusion.2.refs_5_ = bf16[3072,192]{1,0:T(8,128)(2,1)} fusion(bf16[3072,192]{1,0:T(8,128)(2,1)S(1)} %copy-done.38, bf16[48,192]{1,0:T(8,128)(2,1)S(1)} %copy-done.23, s32[192]{0:T(256)S(1)} %copy-done.37, s32[3072]{0:T(1024)S(1)} %get-tuple-element.42, s32[3072]{0:T(1024)S(1)} %copy-done.26), kind=kOutput, calls=%fused_computation.2 | convolution fusion | flops 59129856 | bytes 2403072 | tf_op jit(solution)/shard_map/dot_general | solution.py:139
  70.0 1.4 fusion.9
  72.2 2.3 %copy.101 = bf16[16,128,64]{2,0,1:T(8,128)(2,1)} copy(bf16[16,128,64]{1,0,2:T(8,128)(2,1)} %bitcast.160) | data formatting | bytes 524288 | tf_op jit(solution)/shard_map/reshape | solution.py:163
  76.4 1.4 copy-done
  77.8 33.9 %panel_filter.2 = bf16[2048,64]{1,0:T(8,128)(2,1)S(1)} custom-call(bf16[2240,64]{1,0:T(8,128)(2,1)S(1)} %bitcast.157, bf16[192,3072]{1,0:T(8,128)(2,1)S(1)} %bitcast.154, bf16[1536,256]{1,0:T(8,128)(2,1)S(1)} %bitcast_select_fusion.8.refs_2_, bf16[1536,256]{1,0:T(8,128)(2,1)S(1)} %get-tuple-element.44.refs_3_, ...), custom_call_target="tpu_custom_call" | custom-call | tf_op jit(solution)/shard_map/panel_filter/pallas_call | solution.py:175
  112.5 2.3 %copy.119 = bf16[128,16,64]{0,1,2:T(8,128)(2,1)} copy(bf16[128,16,64]{2,1,0:T(8,128)(2,1)} %bitcast.159) | data formatting | bytes 524288 | tf_op jit(solution)/shard_map/reshape | solution.py:188
  114.8 2.1 %fusion.7 = bf16[16,8,2048]{2,1,0:T(8,128)(2,1)} fusion(bf16[8,8,16,128]{3,2,1,0:T(8,128)(2,1)} %bitcast.162, s32[128]{0:T(128)S(1)} %add_reduce_fusion.1), kind=kOutput, calls=%fused_computation.16 | convolution fusion | flops 33824768 | bytes 786944 | tf_op jit(solution)/shard_map/sc,tc->st/dot_general | solution.py:231
  116.9 6.0 %all-to-all-start.1 = ((bf16[16,8,2048]{2,1,0:T(8,128)(2,1)}), bf16[16,8,2048]{2,1,0:T(8,128)(2,1)}, u32[]{:S(2)}, u32[]{:S(2)}) async-start(bf16[16,8,2048]{2,1,0:T(8,128)(2,1)} %fusion.7), calls=%async_computation.1 | async-start | bytes 1048576 | tf_op jit(solution)/shard_map/all_to_all | solution.py:233
  125.9 2.3 %copy.120 = bf16[16,128,64]{2,0,1:T(8,128)(2,1)} copy(bf16[16,128,64]{1,0,2:T(8,128)(2,1)} %bitcast.161) | data formatting | bytes 524288 | tf_op jit(solution)/shard_map/reshape | solution.py:163
  130.2 1.4 copy-done.1
  131.6 33.7 %panel_filter.3 = bf16[2048,64]{1,0:T(8,128)(2,1)S(1)} custom-call(bf16[2240,64]{1,0:T(8,128)(2,1)S(1)} %bitcast.156, bf16[192,3072]{1,0:T(8,128)(2,1)S(1)} %bitcast.155, bf16[1536,256]{1,0:T(8,128)(2,1)S(1)} %bitcast_select_fusion.8.refs_2_, bf16[1536,256]{1,0:T(8,128)(2,1)S(1)} %get-tuple-element.44.refs_3_, ...), custom_call_target="tpu_custom_call" | custom-call | tf_op jit(solution)/shard_map/panel_filter/pallas_call | solution.py:175
  166.1 1.6 copy.123
  168.9 6.0 %all-to-all-start.3 = ((bf16[16,8,2048]{2,1,0:T(8,128)(2,1)}), bf16[16,8,2048]{2,1,0:T(8,128)(2,1)S(1)}, u32[]{:S(2)}, u32[]{:S(2)}) async-start(bf16[16,8,2048]{2,1,0:T(8,128)(2,1)} %fusion.8), calls=%async_computation.3 | async-start | bytes 1048576 | tf_op jit(solution)/shard_map/all_to_all | solution.py:233
  176.3 13.1 %all-to-all-done.3 = bf16[16,8,2048]{2,1,0:T(8,128)(2,1)S(1)} async-done(((bf16[16,8,2048]{2,1,0:T(8,128)(2,1)}), bf16[16,8,2048]{2,1,0:T(8,128)(2,1)S(1)}, u32[]{:S(2)}, u32[]{:S(2)}) %all-to-all-start.3) | async-done | bytes 524320 | tf_op jit(solution)/shard_map/all_to_all | solution.py:233
  189.4 2.6 %multiply_reduce_fusion = (f32[]{:T(128)}, f32[128,2048]{1,0:T(8,128)S(1)}) fusion(f32[128,2048]{1,0:T(8,128)} %param.10, f32[128,2048]{1,0:T(8,128)} %param.9, f32[128,2048]{1,0:T(8,128)S(1)} %fusion.32, bf16[16,8,2048]{2,1,0:T(8,128)(2,1)S(1)} %all-to-all-done.3, s32[128]{0:T(128)S(1)} %copy-done.29), kind=kOutput, calls=%fused_computation.45 | convolution fusion | flops 68435968 | bytes 4719108 | tf_op jit(solution)/shard_map/sr,st->rt/dot_general | solution.py:234
  192.7 10.3 %all_to_all.25 = f32[16,1,128]{2,1,0:T(1,128)S(1)} all-to-all(f32[16,1,128]{2,1,0:T(1,128)S(1)} %broadcast_in_dim.224), channel_id=1, replica_groups=mesh['line'=2,'bin'=16] {'bin'}, dimensions={0} | all-to-all | bytes 16384 | tf_op jit(solution)/shard_map/all_to_all | solution.py:242
  (139 shorter events, 38.2 us)
Async XLA Ops:
  0.0 17.7 %copy-start.31 = (bf16[3,3,48]{2,1,0:T(4,128)(2,1)S(1)}, bf16[3,3,48]{2,1,0:T(4,128)(2,1)}, u32[]{:S(2)}) copy-start(bf16[3,3,48]{2,1,0:T(4,128)(2,1)} %param.13) | copy-start | bytes 2596
  2.8 13.8 %copy-start.33 = (s32[128]{0:T(128)}, s32[128]{0:T(128)S(1)}, u32[]{:S(2)}) copy-start(s32[128]{0:T(128)S(1)} %compare_select_fusion.1) | copy-start | bytes 1540
  2.9 15.7 %copy-start.16 = (bf16[3,3,48,48]{3,2,1,0:T(8,128)(2,1)S(1)}, bf16[3,3,48,48]{3,2,1,0:T(8,128)(2,1)}, u32[]{:S(2)}) copy-start(bf16[3,3,48,48]{3,2,1,0:T(8,128)(2,1)} %param.14) | copy-start | bytes 124420
  5.1 35.3 %all-to-all-start = ((bf16[16,8,2176]{2,1,0:T(8,128)(2,1)}), bf16[16,8,2176]{2,1,0:T(8,128)(2,1)}, u32[]{:S(2)}, u32[]{:S(2)}) async-start(bf16[16,8,2176]{2,1,0:T(8,128)(2,1)} %fusion), calls=%async_computation | async-start | bytes 1114112 | tf_op jit(solution)/shard_map/all_to_all | solution.py:215
  12.6 5.2 %copy-start.24 = (s32[3072]{0:T(1024)}, s32[3072]{0:T(1024)S(1)}, u32[]{:S(2)}) copy-start(s32[3072]{0:T(1024)S(1)} %get-tuple-element.41) | copy-start | bytes 36868
  25.7 2.5 %copy-start.28 = (s32[128]{0:T(128)S(1)}, s32[128]{0:T(128)}, u32[]{:S(2)}) copy-start(s32[128]{0:T(128)} %get-tuple-element.5) | copy-start | bytes 1540
  25.7 4.6 %copy-start.27 = (s32[512]{0:T(512)S(1)}, s32[512]{0:T(512)}, u32[]{:S(2)}) copy-start(s32[512]{0:T(512)} %add_select_fusion.8) | copy-start | bytes 6148
  27.2 4.9 %copy-start.35 = (s32[256]{0:T(256)S(1)}, s32[256]{0:T(256)}, u32[]{:S(2)}) copy-start(s32[256]{0:T(256)} %and_select_fusion.1) | copy-start | bytes 3076
  27.2 6.0 %copy-start.25 = (s32[3072]{0:T(1024)S(1)}, s32[3072]{0:T(1024)}, u32[]{:S(2)}) copy-start(s32[3072]{0:T(1024)} %copy-done.24) | copy-start | bytes 36868
  28.2 7.9 %copy-start.36 = (s32[192]{0:T(256)}, s32[192]{0:T(256)S(1)}, u32[]{:S(2)}) copy-start(s32[192]{0:T(256)S(1)} %sub.327) | copy-start | bytes 2308
  36.1 3.8 %copy-start.17 = (pred[64,3072]{1,0:T(8,128)(4,1)S(1)}, pred[64,3072]{1,0:T(8,128)(4,1)}, u32[]{:S(2)}) copy-start(pred[64,3072]{1,0:T(8,128)(4,1)} %get-tuple-element.25) | copy-start | bytes 589828
  36.1 3.8 %copy-start.18 = (pred[64,3072]{1,0:T(8,128)(4,1)S(1)}, pred[64,3072]{1,0:T(8,128)(4,1)}, u32[]{:S(2)}) copy-start(pred[64,3072]{1,0:T(8,128)(4,1)} %get-tuple-element.26) | copy-start | bytes 589828
  36.1 3.8 %copy-start.22 = (bf16[3,3072]{1,0:T(4,128)(2,1)S(1)}, bf16[3,3072]{1,0:T(4,128)(2,1)}, u32[]{:S(2)}) copy-start(bf16[3,3072]{1,0:T(4,128)(2,1)} %get-tuple-element.23) | copy-start | bytes 55300
  40.4 9.6 %copy-start.4 = (bf16[1,3,512,256]{2,3,1,0:T(8,128)(2,1)S(1)}, bf16[1,3,512,256]{2,3,1,0:T(8,128)(2,1)}, u32[]{:S(2)}) copy-start(bf16[1,3,512,256]{2,3,1,0:T(8,128)(2,1)} %get-tuple-element.16) | copy-start | bytes 2359300
  40.5 76.4 %all-to-all-start.2 = ((bf16[16,8,2176]{2,1,0:T(8,128)(2,1)}), bf16[16,8,2176]{2,1,0:T(8,128)(2,1)}, u32[]{:S(2)}, u32[]{:S(2)}) async-start(bf16[16,8,2176]{2,1,0:T(8,128)(2,1)} %fusion.1), calls=%async_computation.2 | async-start | bytes 1114112 | tf_op jit(solution)/shard_map/all_to_all | solution.py:215
  52.4 2.5 %copy-start.6 = (bf16[1,3,512,256]{2,3,1,0:T(8,128)(2,1)S(1)}, bf16[1,3,512,256]{2,3,1,0:T(8,128)(2,1)}, u32[]{:S(2)}) copy-start(bf16[1,3,512,256]{2,3,1,0:T(8,128)(2,1)} %get-tuple-element.10) | copy-start | bytes 2359300
  52.4 3.6 %copy-start.5 = (bf16[1,3,512,256]{2,3,1,0:T(8,128)(2,1)S(1)}, bf16[1,3,512,256]{2,3,1,0:T(8,128)(2,1)}, u32[]{:S(2)}) copy-start(bf16[1,3,512,256]{2,3,1,0:T(8,128)(2,1)} %get-tuple-element.8) | copy-start | bytes 2359300
  54.8 2.4 %copy-start.9 = (bf16[1,3,512,256]{2,3,1,0:T(8,128)(2,1)S(1)}, bf16[1,3,512,256]{2,3,1,0:T(8,128)(2,1)}, u32[]{:S(2)}) copy-start(bf16[1,3,512,256]{2,3,1,0:T(8,128)(2,1)} %get-tuple-element.12) | copy-start | bytes 2359300
  56.0 2.4 %copy-start.8 = (bf16[1,3,512,256]{2,3,1,0:T(8,128)(2,1)S(1)}, bf16[1,3,512,256]{2,3,1,0:T(8,128)(2,1)}, u32[]{:S(2)}) copy-start(bf16[1,3,512,256]{2,3,1,0:T(8,128)(2,1)} %get-tuple-element.13) | copy-start | bytes 2359300
  57.2 2.3 %copy-start.7 = (bf16[1,3,512,256]{2,3,1,0:T(8,128)(2,1)S(1)}, bf16[1,3,512,256]{2,3,1,0:T(8,128)(2,1)}, u32[]{:S(2)}) copy-start(bf16[1,3,512,256]{2,3,1,0:T(8,128)(2,1)} %get-tuple-element.11) | copy-start | bytes 2359300
  58.4 2.3 %copy-start.30 = (bf16[48,3]{0,1:T(4,128)(2,1)S(1)}, bf16[48,3]{0,1:T(4,128)(2,1)}, u32[]{:S(2)}) copy-start(bf16[48,3]{0,1:T(4,128)(2,1)} %get-tuple-element.27) | copy-start | bytes 868
  58.4 3.3 %copy-start.14 = (bf16[1,3,512,256]{3,2,1,0:T(8,128)(2,1)S(1)}, bf16[1,3,512,256]{3,2,1,0:T(8,128)(2,1)}, u32[]{:S(2)}) copy-start(bf16[1,3,512,256]{3,2,1,0:T(8,128)(2,1)} %copy.106) | copy-start | bytes 2359300
  61.7 2.2 %copy-start.20 = (pred[512,256]{1,0:T(8,128)(4,1)S(1)}, pred[512,256]{1,0:T(8,128)(4,1)}, u32[]{:S(2)}) copy-start(pred[512,256]{1,0:T(8,128)(4,1)} %get-tuple-element.31) | copy-start | bytes 393220
  61.7 2.3 %copy-start.21 = (pred[512,256]{1,0:T(8,128)(4,1)S(1)}, pred[512,256]{1,0:T(8,128)(4,1)}, u32[]{:S(2)}) copy-start(pred[512,256]{1,0:T(8,128)(4,1)} %get-tuple-element.32) | copy-start | bytes 393220
  64.0 2.5 %copy-start.23 = (bf16[48,192]{1,0:T(8,128)(2,1)S(1)}, bf16[48,192]{1,0:T(8,128)(2,1)}, u32[]{:S(2)}) copy-start(bf16[48,192]{1,0:T(8,128)(2,1)} %reshape.664) | copy-start | bytes 55300
  64.0 2.5 %copy-start.26 = (s32[3072]{0:T(1024)S(1)}, s32[3072]{0:T(1024)}, u32[]{:S(2)}) copy-start(s32[3072]{0:T(1024)} %copy-done.24) | copy-start | bytes 36868
  64.0 2.5 %copy-start.37 = (s32[192]{0:T(256)S(1)}, s32[192]{0:T(256)}, u32[]{:S(2)}) copy-start(s32[192]{0:T(256)} %copy-done.36) | copy-start | bytes 2308
  64.0 2.5 %copy-start.38 = (bf16[3072,192]{1,0:T(8,128)(2,1)S(1)}, bf16[3072,192]{1,0:T(8,128)(2,1)}, u32[]{:S(2)}) copy-start(bf16[3072,192]{1,0:T(8,128)(2,1)} %convolution_select_fusion.1) | copy-start | bytes 3538948
  116.9 52.0 %all-to-all-start.1 = ((bf16[16,8,2048]{2,1,0:T(8,128)(2,1)}), bf16[16,8,2048]{2,1,0:T(8,128)(2,1)}, u32[]{:S(2)}, u32[]{:S(2)}) async-start(bf16[16,8,2048]{2,1,0:T(8,128)(2,1)} %fusion.7), calls=%async_computation.1 | async-start | bytes 1048576 | tf_op jit(solution)/shard_map/all_to_all | solution.py:233
  166.1 8.8 %copy-start.34 = (s32[128]{0:T(128)S(1)}, s32[128]{0:T(128)}, u32[]{:S(2)}) copy-start(s32[128]{0:T(128)} %copy-done.33) | copy-start | bytes 1540
  167.8 21.6 %copy-start.29 = (s32[128]{0:T(128)S(1)}, s32[128]{0:T(128)}, u32[]{:S(2)}) copy-start(s32[128]{0:T(128)} %get-tuple-element.5) | copy-start | bytes 1540
  168.9 20.4 %all-to-all-start.3 = ((bf16[16,8,2048]{2,1,0:T(8,128)(2,1)}), bf16[16,8,2048]{2,1,0:T(8,128)(2,1)S(1)}, u32[]{:S(2)}, u32[]{:S(2)}) async-start(bf16[16,8,2048]{2,1,0:T(8,128)(2,1)} %fusion.8), calls=%async_computation.3 | async-start | bytes 1048576 | tf_op jit(solution)/shard_map/all_to_all | solution.py:233
  (11 other events, 18.0 us)

commit v3 on v2

--- a/solution.py
+++ b/solution.py
@@ -116,44 +116,109 @@
     return max(d for d in range(1, most + 1) if blocks % d == 0)
 
 
+def by_chan(v):
+    return (v * 43691) >> 21
+
+
+def one_hot(remainder, index, value):
+    return jnp.where(remainder == index, value, 0.0).astype(jnp.bfloat16)
+
+
+def weights_body(
+    conv_in_ref,
+    conv_mid_ref,
+    conv_out_ref,
+    w_in_ref,
+    w_mid0_ref,
+    w_mid1_ref,
+    w_mid2_ref,
+    w_out_ref,
+):
+    f32 = jnp.float32
+
+    def iota(shape, axis):
+        return lax.broadcasted_iota(jnp.int32, shape, axis)
+
+    def offset_of(place):
+        return jnp.where(place < OFFS // 2, 2 * place, 2 * place - OFFS + 1)
+
+    others = iota((OFFS, 1), 0) + 1
+
+    @pl.loop(0, 6)
+    def _(part):
+        base = pl.multiple_of(part * 512, 512)
+        lane = iota((1, 512), 1) + base
+        place = by_chan(lane)
+        near = others - offset_of(place)
+        spread = one_hot(lane - CHAN * place, iota((CHAN, 1), 0), 0.5)
+        wide = [jnp.dot(conv_in_ref[a], spread, preferred_element_type=f32) for a in range(3)]
+        for d in range(3):
+            value = jnp.zeros((OFFS, 512), f32)
+            for a in range(3):
+                value = jnp.where(near == a, wide[a][d : d + 1, :], value)
+            w_in_ref[pl.ds(d * OFFS, OFFS), pl.ds(base, 512)] = value.astype(jnp.bfloat16)
+
+    for m, w_mid_ref in enumerate((w_mid0_ref, w_mid1_ref, w_mid2_ref)):
+        x = iota((512, 1), 0) + (256 * m - 128 + 3 * CHAN)
+        y = iota((1, TILE), 1) + 256 * m
+        cell_x = by_chan(x)
+        cell_y = by_chan(y)
+        rows = one_hot(x - CHAN * cell_x, iota((1, CHAN), 1), 1.0)
+        cols = one_hot(y - CHAN * cell_y, iota((CHAN, 1), 0), 0.5)
+        wide = jnp.dot(conv_mid_ref[...], cols, preferred_element_type=f32)
+        wide = wide.astype(jnp.bfloat16)
+        tap = cell_x - 2 - cell_y
+        for d in range(3):
+            value = jnp.zeros((512, TILE), f32)
+            for a in range(3):
+                start = (a * 3 + d) * CHAN
+                part = jnp.dot(
+                    rows, wide[start : start + CHAN, :], preferred_element_type=f32
+                )
+                value = jnp.where(tap == a, part, value)
+            w_mid_ref[pl.ds(d * 512, 512), :] = value.astype(jnp.bfloat16)
+
+    triple = iota((1, 3 * OFFS), 1)
+    group = triple // OFFS
+    wide_out = []
+    for a in range(3):
+        value = jnp.zeros((CHAN, 3 * OFFS), f32)
+        for d in range(3):
+            value = jnp.where(group == d, conv_out_ref[a, :, d : d + 1].astype(f32), value)
+        wide_out.append(value.astype(jnp.bfloat16))
+
+    @pl.loop(0, 6)
+    def _(part):
+        base = pl.multiple_of(part * 512, 512)
+        lane = iota((512, 1), 0) + base
+        place = by_chan(lane)
+        near = offset_of(place) + 1 - (triple - OFFS * group)
+        across = one_hot(lane - CHAN * place, iota((1, CHAN), 1), 1.0)
+        value = jnp.zeros((512, 3 * OFFS), f32)
+        for a in range(3):
+            value = jnp.where(
+                near == a, jnp.dot(across, wide_out[a], preferred_element_type=f32), value
+            )
+        w_out_ref[pl.ds(base, 512), :] = value.astype(jnp.bfloat16)
+
+
 def band_weights(conv_in, conv_mid, conv_out):
-    lane = jnp.arange(OFFS * CHAN)
-    place = lane // CHAN
-    offset = 2 * (place % (OFFS // 2)) + place // (OFFS // 2)
-    spread = (jnp.arange(CHAN)[:, None] == (lane % CHAN)[None]).astype(jnp.bfloat16)
-    zero = jnp.bfloat16(0)
-    half = jnp.bfloat16(0.5)
-    others = jnp.arange(OFFS)
-
-    near = others[:, None] - offset[None, :] + 1
-    wide_in = jnp.dot((conv_in * half).reshape(9, CHAN), spread).reshape(3, 3, 1, OFFS * CHAN)
-    w_in = zero
-    for a in range(3):
-        w_in = jnp.where((near == a)[None], wide_in[a], w_in)
-    w_in = w_in.reshape(3 * OFFS, OFFS * CHAN)
-
-    near = offset[:, None] - jnp.tile(others, 3)[None, :] + 1
-    w_out = zero
-    for a in range(3):
-        w_out = jnp.where(
-            near == a, jnp.dot(spread.T, jnp.repeat(conv_out[a].T, OFFS, axis=1)), w_out
-        )
-
-    scaled = conv_mid * half
-    tiles = []
-    for m in range(3):
-        x = jnp.arange(512) + 256 * m - 128
-        y = jnp.arange(256) + 256 * m
-        rows = (x[:, None] % CHAN == jnp.arange(CHAN)[None]).astype(jnp.bfloat16)
-        cols = (jnp.arange(CHAN)[:, None] == y[None] % CHAN).astype(jnp.bfloat16)
-        tap = (x // CHAN)[:, None] - (y // CHAN)[None] + 1
-        wide = jnp.einsum("adce,ey->adcy", scaled, cols)
-        wide = jnp.einsum("xc,adcy->adxy", rows, wide)
-        banded = jnp.where(tap[None] == 0, wide[0], zero)
-        banded = jnp.where(tap[None] == 1, wide[1], banded)
-        banded = jnp.where(tap[None] == 2, wide[2], banded)
-        tiles.append(banded.reshape(1536, 256))
-    return w_in, tiles[0], tiles[1], tiles[2], w_out
+    bf16 = jnp.bfloat16
+    mid = jax.ShapeDtypeStruct((1536, TILE), bf16)
+    return pl.pallas_call(
+        weights_body,
+        out_shape=(
+            jax.ShapeDtypeStruct((3 * OFFS, OFFS * CHAN), bf16),
+            mid,
+            mid,
+            mid,
+            jax.ShapeDtypeStruct((OFFS * CHAN, 3 * OFFS), bf16),
+        ),
+        in_specs=[pl.BlockSpec(memory_space=pltpu.VMEM)] * 3,
+        out_specs=[pl.BlockSpec(memory_space=pltpu.VMEM)] * 5,
+        compiler_params=pltpu.CompilerParams(vmem_limit_bytes=40 * 1024 * 1024),
+        name="band_weights",
+    )(conv_in, conv_mid.reshape(9 * CHAN, CHAN), conv_out.transpose(0, 2, 1))
 
 
 def filter_rows(panel, weights):
@@ -212,11 +277,17 @@
         pick = (slot_index[:, None] == send_slot[None, :]).astype(jnp.bfloat16)
         outgoing = jnp.dot(pick, labelled, preferred_element_type=jnp.float32)
         outgoing = outgoing.astype(jnp.bfloat16).reshape(owners, capacity, samples + 128)
+        if b == 0:
+            outgoing, conv_in, conv_mid, conv_out = lax.optimization_barrier(
+                (outgoing, conv_in, conv_mid, conv_out)
+            )
+            weights = band_weights(conv_in, conv_mid, conv_out)
+        else:
+            outgoing, weights = lax.optimization_barrier((outgoing, weights))
         arrived = lax.all_to_all(outgoing, "bin", split_axis=0, concat_axis=0, tiled=True)
         picks.append(pick)
         arrivals.append(arrived.reshape(slots, samples + 128))
 
-    weights = band_weights(conv_in, conv_mid, conv_out)
     own_rows = 0.0
     for b in range(bin_dev):
         cell = arrivals[b][:, samples].astype(jnp.int32) - 1

time: 207 us -> 169 us (0.82)
  local copies, waits for them, and re-layouts: 37.6 us -> 21.1 us
  other arithmetic: 22.1 us -> 7.79 us
  matrix products: 27.8 us -> 14.4 us
  Pallas kernels: 67.7 us -> 73.4 us
  waiting for transfers between devices: 13.1 us -> 15.8 us
    slice x13 -> x0, local copies, waits for them, and re-layouts: 18 us -> none  [the longest x6 7.91 us: band_weights(): banded = jnp.where(tap[None] == 2, wide[2], banded)]
    dot_general x7 -> x0, matrix products: 13.4 us -> none  [the longest x3 9.03 us: band_weights(): jnp.dot(spread.T, jnp.repeat(conv_out[a].T, OFFS, axis=1))]
    select_n x16 -> x0, other arithmetic: 8.73 us -> none  [the longest x2 4.2 us: band_weights(): banded = jnp.where(tap[None] == 2, wide[2], banded)]
    pallas_call x0 -> x1, Pallas kernels: none -> 5.98 us  [band_weights(): pl.pallas_call(weights_body, out_shape=(jax.ShapeDtypeStruct((3 * OFFS, O...]
    eq x4 -> x0, other arithmetic: 4.99 us -> none  [the longest x3 3.88 us: band_weights(): banded = jnp.where(tap[None] == 2, wide[2], banded)]
    unnamed x80 -> x28, local copies, waits for them, and re-layouts: 6.53 us -> 9.43 us
    all_to_all x2, waiting for transfers between devices: 0.01 us -> 2.71 us  [local(): lax.all_to_all(outgoing, 'bin', split_axis=0, concat_axis=0, tiled=True)]
  transfers between devices with their start and end apart: 4 -> 4, of which waited for: 1 -> 2; matrix products, arithmetic and copies ran while one was open for 35% -> 16% of each run, Pallas kernels for 33% -> 44%
where the time goes in v3:
time: 169 us; the launch traced here: 167 us
  Pallas kernels  73.4 us (43%)
  starting transfers between devices  23.7 us (14%)
  local copies, waits for them, and re-layouts  21.1 us (12%)
  waiting for transfers between devices  15.8 us (9%)
  matrix products  14.4 us (9%)
  blocking collectives  10.3 us (6%)
  other arithmetic  7.79 us (5%)
    pallas_call x2, Pallas kernels, filter_rows(): pl.pallas_call(body, out_shape=jax.ShapeDtypeStruct((span * blk, offs), j...  67.5 us
    all_to_all x2, waiting for transfers between devices, local(): lax.all_to_all(answer, 'bin', split_axis=0, concat_axis=0, tiled=True)  13.1 us
    all_to_all x2, starting transfers between devices, local(): lax.all_to_all(outgoing, 'bin', split_axis=0, concat_axis=0, tiled=True)  11.8 us
    all_to_all x2, starting transfers between devices, local(): lax.all_to_all(answer, 'bin', split_axis=0, concat_axis=0, tiled=True)  11.8 us
    all_to_all x1, blocking collectives, local(): lax.all_to_all(share, 'bin', split_axis=0, concat_axis=0, tiled=True)  10.3 us
    unnamed x28, local copies, waits for them, and re-layouts  9.43 us
    pallas_call x1, Pallas kernels, band_weights(): pl.pallas_call(weights_body, out_shape=(jax.ShapeDtypeStruct((3 * OFFS, O...  5.98 us
    reshape x2, local copies, waits for them, and re-layouts, filter_rows(): segs = panel.reshape(SEGS, span, offs)  4.55 us
  transfers between devices with their start and end apart: 4, of which 2 were waited for; matrix products, arithmetic and copies ran while one was open for 16% of the time, Pallas kernels for 44%

profile of v3, /device:TPU:0, one launch (start us, length us, event | category | flops | bytes accessed | tf_op | source)
XLA Modules:
  0.0 167.3 jit_solution(12916859024690388969)
XLA Ops:
  0.7 0.9 convert_reduce_fusion
  3.0 2.2 %fusion = bf16[16,8,2176]{2,1,0:T(8,128)(2,1)} fusion(bf16[128,128]{1,0:T(8,128)(2,1)S(1)} %broadcast_in_dim.6, bf16[128,2048]{1,0:T(8,128)(2,1)} %param.8, s32[128]{0:T(128)S(1)} %compare_select_fusion.1), kind=kOutput, calls=%fused_computation.2 | convolution fusion | flops 72712192 | bytes 1114624 | tf_op jit(solution)/shard_map/dot_general | solution.py:278
  5.1 7.4 %all-to-all-start = ((bf16[16,8,2176]{2,1,0:T(8,128)(2,1)}), bf16[16,8,2176]{2,1,0:T(8,128)(2,1)}, u32[]{:S(2)}, u32[]{:S(2)}) async-start(bf16[16,8,2176]{2,1,0:T(8,128)(2,1)} %fusion), calls=%async_computation | async-start | bytes 1114112 | tf_op jit(solution)/shard_map/all_to_all | solution.py:287
  14.1 0.9 copy-done.9
  15.0 6.0 %band_weights.1 = (bf16[192,3072]{1,0:T(8,128)(2,1)S(1)}, bf16[1536,256]{1,0:T(8,128)(2,1)S(1)}, bf16[1536,256]{1,0:T(8,128)(2,1)S(1)}, bf16[1536,256]{1,0:T(8,128)(2,1)S(1)}, bf16[3072,192]{1,0:T(8,128)(2,1)S(1)}) custom-call(bf16[3,3,48]{2,1,0:T(4,128)(2,1)S(1)} %copy-done.10, bf16[432,48]{1,0:T(8,128)(2,1)S(1)} %bitcast.57, bf16[3,48,3]{2,1,0:T(8,128)(2,1)S(1)} %bitcast.56), custom_call_target="tpu_custom_call" | custom-call | tf_op jit(solution)/shard_map/band_weights/pallas_call | solution.py:208
  21.0 0.9 copy-done
  21.8 0.9 copy-done.3
  22.8 2.2 %fusion.1 = bf16[16,8,2176]{2,1,0:T(8,128)(2,1)} fusion(bf16[128,128]{1,0:T(8,128)(2,1)} %copy-done.11, bf16[128,2048]{1,0:T(8,128)(2,1)} %param.8, s32[128]{0:T(128)S(1)} %get-tuple-element.35), kind=kOutput, calls=%fused_computation.3 | convolution fusion | flops 72712192 | bytes 1114624 | tf_op jit(solution)/shard_map/dot_general | solution.py:278
  24.9 2.7 %all-to-all-done = bf16[16,8,2176]{2,1,0:T(8,128)(2,1)} async-done(((bf16[16,8,2176]{2,1,0:T(8,128)(2,1)}), bf16[16,8,2176]{2,1,0:T(8,128)(2,1)}, u32[]{:S(2)}, u32[]{:S(2)}) %all-to-all-start) | async-done | bytes 557088 | tf_op jit(solution)/shard_map/all_to_all | solution.py:287
  27.6 4.4 %all-to-all-start.2 = ((bf16[16,8,2176]{2,1,0:T(8,128)(2,1)}), bf16[16,8,2176]{2,1,0:T(8,128)(2,1)}, u32[]{:S(2)}, u32[]{:S(2)}) async-start(bf16[16,8,2176]{2,1,0:T(8,128)(2,1)} %fusion.1), calls=%async_computation.2 | async-start | bytes 1114112 | tf_op jit(solution)/shard_map/all_to_all | solution.py:287
  32.1 0.9 add_reduce_fusion.1
  33.0 1.4 fusion.6
  35.1 2.3 %copy.45 = bf16[16,128,64]{2,0,1:T(8,128)(2,1)} copy(bf16[16,128,64]{1,0,2:T(8,128)(2,1)} %bitcast.58) | data formatting | bytes 524288 | tf_op jit(solution)/shard_map/reshape | solution.py:228
  38.2 1.2 fusion.13
  39.4 1.1 copy-done.4
  40.5 33.7 %panel_filter.2 = bf16[2048,64]{1,0:T(8,128)(2,1)S(1)} custom-call(bf16[2240,64]{1,0:T(8,128)(2,1)S(1)} %bitcast.53, bf16[192,3072]{1,0:T(8,128)(2,1)S(1)} %get-tuple-element.29.refs_1_, bf16[1536,256]{1,0:T(8,128)(2,1)S(1)} %get-tuple-element.30.refs_2_, bf16[1536,256]{1,0:T(8,128)(2,1)S(1)} %copy-done.1, bf16[1536,256]{1,0:T(8,128)(2,1)S(1)} %copy-done.4, ...), custom_call_target="tpu_custom_call" | custom-call | tf_op jit(solution)/shard_map/panel_filter/pallas_call | solution.py:240
  75.1 2.3 %copy.49 = bf16[128,16,64]{0,1,2:T(8,128)(2,1)} copy(bf16[128,16,64]{2,1,0:T(8,128)(2,1)} %bitcast.55) | data formatting | bytes 524288 | tf_op jit(solution)/shard_map/reshape | solution.py:253
  77.4 2.1 %fusion.4 = bf16[16,8,2048]{2,1,0:T(8,128)(2,1)} fusion(bf16[8,8,16,128]{3,2,1,0:T(8,128)(2,1)} %bitcast.60, s32[128]{0:T(128)S(1)} %add_reduce_fusion.1), kind=kOutput, calls=%fused_computation.9 | convolution fusion | flops 33824768 | bytes 786944 | tf_op jit(solution)/shard_map/sc,tc->st/dot_general | solution.py:302
  79.5 5.9 %all-to-all-start.1 = ((bf16[16,8,2048]{2,1,0:T(8,128)(2,1)}), bf16[16,8,2048]{2,1,0:T(8,128)(2,1)}, u32[]{:S(2)}, u32[]{:S(2)}) async-start(bf16[16,8,2048]{2,1,0:T(8,128)(2,1)} %fusion.4), calls=%async_computation.1 | async-start | bytes 1048576 | tf_op jit(solution)/shard_map/all_to_all | solution.py:304
  86.2 1.4 fusion.7
  88.4 2.3 %copy.50 = bf16[16,128,64]{2,0,1:T(8,128)(2,1)} copy(bf16[16,128,64]{1,0,2:T(8,128)(2,1)} %bitcast.59) | data formatting | bytes 524288 | tf_op jit(solution)/shard_map/reshape | solution.py:228
  91.5 1.2 fusion.15
  92.7 1.1 copy-done.5
  93.8 33.7 %panel_filter.3 = bf16[2048,64]{1,0:T(8,128)(2,1)S(1)} custom-call(bf16[2240,64]{1,0:T(8,128)(2,1)S(1)} %bitcast.52, bf16[192,3072]{1,0:T(8,128)(2,1)S(1)} %get-tuple-element.29.refs_1_, bf16[1536,256]{1,0:T(8,128)(2,1)S(1)} %get-tuple-element.30.refs_2_, bf16[1536,256]{1,0:T(8,128)(2,1)S(1)} %copy-done.2, bf16[1536,256]{1,0:T(8,128)(2,1)S(1)} %copy-done.5, ...), custom_call_target="tpu_custom_call" | custom-call | tf_op jit(solution)/shard_map/panel_filter/pallas_call | solution.py:240
  128.3 1.6 copy.53
  130.0 1.1 fusion.5
  131.1 5.9 %all-to-all-start.3 = ((bf16[16,8,2048]{2,1,0:T(8,128)(2,1)}), bf16[16,8,2048]{2,1,0:T(8,128)(2,1)S(1)}, u32[]{:S(2)}, u32[]{:S(2)}) async-start(bf16[16,8,2048]{2,1,0:T(8,128)(2,1)} %fusion.5), calls=%async_computation.3 | async-start | bytes 1048576 | tf_op jit(solution)/shard_map/all_to_all | solution.py:304
  137.1 1.4 fusion.19
  138.4 13.1 %all-to-all-done.3 = bf16[16,8,2048]{2,1,0:T(8,128)(2,1)S(1)} async-done(((bf16[16,8,2048]{2,1,0:T(8,128)(2,1)}), bf16[16,8,2048]{2,1,0:T(8,128)(2,1)S(1)}, u32[]{:S(2)}, u32[]{:S(2)}) %all-to-all-start.3) | async-done | bytes 524320 | tf_op jit(solution)/shard_map/all_to_all | solution.py:304
  151.5 2.6 %multiply_reduce_fusion = (f32[]{:T(128)}, f32[128,2048]{1,0:T(8,128)S(1)}) fusion(f32[128,2048]{1,0:T(8,128)} %param.10, f32[128,2048]{1,0:T(8,128)} %param.9, f32[128,2048]{1,0:T(8,128)S(1)} %fusion.19, bf16[16,8,2048]{2,1,0:T(8,128)(2,1)S(1)} %all-to-all-done.3, s32[128]{0:T(128)S(1)} %get-tuple-element.35), kind=kOutput, calls=%fused_computation.22 | convolution fusion | flops 68435968 | bytes 4719108 | tf_op jit(solution)/shard_map/sr,st->rt/dot_general | solution.py:305
  154.8 10.3 %all_to_all.25 = f32[16,1,128]{2,1,0:T(1,128)S(1)} all-to-all(f32[16,1,128]{2,1,0:T(1,128)S(1)} %broadcast_in_dim.7), channel_id=1, replica_groups=mesh['line'=2,'bin'=16] {'bin'}, dimensions={0} | all-to-all | bytes 16384 | tf_op jit(solution)/shard_map/all_to_all | solution.py:313
  166.4 0.9 multiply_convert_fusion
  (35 shorter events, 10.5 us)
Async XLA Ops:
  0.0 12.5 %copy-start.12 = (bf16[3,3,48]{2,1,0:T(4,128)(2,1)S(1)}, bf16[3,3,48]{2,1,0:T(4,128)(2,1)}, u32[]{:S(2)}) copy-start(bf16[3,3,48]{2,1,0:T(4,128)(2,1)} %param.15) | copy-start | bytes 2596
  2.3 11.0 %copy-start.10 = (bf16[3,3,48]{2,1,0:T(4,128)(2,1)S(1)}, bf16[3,3,48]{2,1,0:T(4,128)(2,1)}, u32[]{:S(2)}) copy-start(bf16[3,3,48]{2,1,0:T(4,128)(2,1)} %conv_in_ref) | copy-start | bytes 2596
  2.4 0.6 copy-start.11
  5.1 22.5 %all-to-all-start = ((bf16[16,8,2176]{2,1,0:T(8,128)(2,1)}), bf16[16,8,2176]{2,1,0:T(8,128)(2,1)}, u32[]{:S(2)}, u32[]{:S(2)}) async-start(bf16[16,8,2176]{2,1,0:T(8,128)(2,1)} %fusion), calls=%async_computation | async-start | bytes 1114112 | tf_op jit(solution)/shard_map/all_to_all | solution.py:287
  13.3 0.8 copy-start.8
  14.1 0.9 copy-start.9
  20.9 0.9 copy-start
  21.8 0.9 copy-start.3
  27.6 51.9 %all-to-all-start.2 = ((bf16[16,8,2176]{2,1,0:T(8,128)(2,1)}), bf16[16,8,2176]{2,1,0:T(8,128)(2,1)}, u32[]{:S(2)}, u32[]{:S(2)}) async-start(bf16[16,8,2176]{2,1,0:T(8,128)(2,1)} %fusion.1), calls=%async_computation.2 | async-start | bytes 1114112 | tf_op jit(solution)/shard_map/all_to_all | solution.py:287
  37.4 2.0 %copy-start.1 = (bf16[1536,256]{1,0:T(8,128)(2,1)S(1)}, bf16[1536,256]{1,0:T(8,128)(2,1)}, u32[]{:S(2)}) copy-start(bf16[1536,256]{1,0:T(8,128)(2,1)} %copy-done) | copy-start | bytes 2359300
  39.4 1.1 copy-start.4
  74.3 0.8 copy-start.7
  79.5 51.6 %all-to-all-start.1 = ((bf16[16,8,2048]{2,1,0:T(8,128)(2,1)}), bf16[16,8,2048]{2,1,0:T(8,128)(2,1)}, u32[]{:S(2)}, u32[]{:S(2)}) async-start(bf16[16,8,2048]{2,1,0:T(8,128)(2,1)} %fusion.4), calls=%async_computation.1 | async-start | bytes 1048576 | tf_op jit(solution)/shard_map/all_to_all | solution.py:304
  90.7 2.0 %copy-start.2 = (bf16[1536,256]{1,0:T(8,128)(2,1)S(1)}, bf16[1536,256]{1,0:T(8,128)(2,1)}, u32[]{:S(2)}) copy-start(bf16[1536,256]{1,0:T(8,128)(2,1)} %copy-done) | copy-start | bytes 2359300
  92.7 1.1 copy-start.5
  127.5 0.8 copy-start.6
  131.1 20.4 %all-to-all-start.3 = ((bf16[16,8,2048]{2,1,0:T(8,128)(2,1)}), bf16[16,8,2048]{2,1,0:T(8,128)(2,1)S(1)}, u32[]{:S(2)}, u32[]{:S(2)}) async-start(bf16[16,8,2048]{2,1,0:T(8,128)(2,1)} %fusion.5), calls=%async_computation.3 | async-start | bytes 1048576 | tf_op jit(solution)/shard_map/all_to_all | solution.py:304
